TPU v7x, 32 devices: a whole 2x2x4 slice. The times are simulated.
32 devices in a mesh: tm: 8 (over y, x, core), elem: 4 (over z).
Axes of the slice: x: 2, y: 2, z: 4, core: 2. Of those that a mesh axis runs over, the one named last changes fastest.
Arguments:
- samples: float32 [2, 512, 24576], P(None, 'elem', 'tm'), may hold values from -24 to 24
- shift_bin: int32 [1], replicated, may hold values from 1 to 63
- start_vectors: int32 [2, 512, 64], P(None, 'elem'), may hold values from 0 to 8
- tap_table: int32 [4, 1024], replicated, may hold values from -2048 to 2047
Outputs:
- spectra: float32 [2, 64, 24, 1024], P(None, 'elem', 'tm')
- weights: float32 [2, 512, 64], P(None, 'elem')
All inputs are finite; a program needn't handle non-finite values.
Results may differ from a plain program's by a relative error of at most 0.0003.
Values sent between devices are 32-bit elements; how exact they have to be, the bound alone decides.
No kernel may reach another device: no remote copies, remote signals or barrier semaphores. Data moves between devices by JAX's collectives and lax.ppermute only.
A program may use at most 128 MiB of HBM per device.

v0:
```python
import math

import jax
import jax.numpy as jnp
from jax import lax
from jax.sharding import PartitionSpec as P

ELEMS = 512
BEAMS = 64
CHANNELS = 1024
TAPS = 4
ITERS = 3


EPS = 1e-06
HIGH = lax.Precision.HIGHEST


def from_behind(x, axis, by):
    devices = lax.axis_size(axis)
    pairs = [(i, i + by) for i in range(devices) if 0 <= i + by < devices]
    return lax.ppermute(x, axis, pairs)


def rotation(shift_bin, offset, count, modulus):
    times = offset + lax.iota(jnp.int32, count)
    folded = shift_bin[0] * times % modulus
    angle = 2.0 * math.pi / modulus * folded.astype(jnp.float32)
    return (jnp.cos(angle), jnp.sin(angle))


def stacked_left(sig_real, sig_imag, cos_table, sin_table):
    mod_real = sig_real * cos_table + sig_imag * sin_table
    mod_imag = sig_imag * cos_table - sig_real * sin_table
    return jnp.concatenate([sig_real, sig_imag, mod_real, mod_imag], 0)


def contract(left_rows, right_rows):
    return lax.dot_general(
        left_rows,
        right_rows,
        (((1,), (1,)), ((), ())),
        precision=HIGH,
        preferred_element_type=jnp.float32,
    )


def transposed(left_rows, right_rows):
    return lax.dot_general(
        left_rows,
        right_rows,
        (((0,), (0,)), ((), ())),
        precision=HIGH,
        preferred_element_type=jnp.float32,
    )


def matmul(left_rows, right_rows):
    return jnp.dot(left_rows, right_rows, precision=HIGH, preferred_element_type=jnp.float32)


def correlate(left_rows, right_pair, row_count):
    right_rows = jnp.concatenate([right_pair[0], right_pair[1]], 0)
    grams = contract(left_rows, right_rows)
    col_count = right_pair.shape[1]

    def block(row_block, col_block):
        return grams[
            row_block * row_count : (row_block + 1) * row_count,
            col_block * col_count : (col_block + 1) * col_count,
        ]

    return jnp.stack(
        [
            block(0, 0) + block(1, 1),
            block(1, 0) - block(0, 1),
            block(2, 0) + block(3, 1),
            block(3, 0) - block(2, 1),
        ]
    )


def column_squares(vector):
    return jnp.sum(vector * vector, axis=(0, 1))


def column_norms(vector):
    return lax.psum(column_squares(vector), "elem")


def body(samples, shift_bin, start_vectors, tap_table):
    span_len = samples.shape[2]
    elem_count = lax.axis_size("elem")
    modulus = span_len * lax.axis_size("tm")
    elems_dev = samples.shape[1]
    span_start = lax.axis_index("tm") * span_len
    regrouped = lax.all_to_all(samples, "elem", split_axis=2, concat_axis=1, tiled=True)
    quarter = span_len // elem_count
    cos_table, sin_table = rotation(
        shift_bin, span_start + lax.axis_index("elem") * quarter, quarter, modulus
    )
    left_rows = stacked_left(regrouped[0], regrouped[1], cos_table, sin_table)
    full_corr = correlate(left_rows, regrouped, ELEMS)
    partial_corr = lax.psum_scatter(full_corr, "elem", scatter_dimension=1, tiled=True)
    summed_corr = lax.psum(partial_corr, "tm")
    plain_real = summed_corr[0] / modulus
    plain_imag = summed_corr[1] / modulus
    cyc_scale = 1.0 / math.sqrt(modulus * ELEMS)
    cyc_real = summed_corr[2] * cyc_scale
    cyc_imag = summed_corr[3] * cyc_scale
    row_start = lax.axis_index("elem") * elems_dev
    initial = start_vectors.astype(jnp.float32) - 4.5
    vector = initial / jnp.sqrt(column_norms(initial) + EPS)
    for iteration in range(ITERS):
        adjoint_vec_real = vector[0]
        adjoint_vec_imag = vector[1]
        adj_real = transposed(cyc_real, adjoint_vec_real) + transposed(cyc_imag, adjoint_vec_imag)
        adj_imag = transposed(cyc_real, adjoint_vec_imag) - transposed(cyc_imag, adjoint_vec_real)
        herm_real = transposed(plain_real, adjoint_vec_real) + transposed(
            plain_imag, adjoint_vec_imag
        )
        herm_imag = transposed(plain_real, adjoint_vec_imag) - transposed(
            plain_imag, adjoint_vec_real
        )
        summed = lax.psum(jnp.stack([adj_real, adj_imag, herm_real, herm_imag]), "elem")
        own_plain = lax.dynamic_slice_in_dim(summed[2:4], row_start, elems_dev, 1)
        out_real = matmul(cyc_real, summed[0]) - matmul(cyc_imag, summed[1]) + own_plain[0]
        out_imag = matmul(cyc_real, summed[1]) + matmul(cyc_imag, summed[0]) + own_plain[1]
        vector = jnp.stack([out_real, out_imag])
        vector = vector / jnp.sqrt(column_norms(vector) + EPS)
    vec_real, vec_imag = (vector[0], vector[1])
    beam_real = transposed(vec_real, samples[0]) + transposed(vec_imag, samples[1])
    beam_imag = transposed(vec_real, samples[1]) - transposed(vec_imag, samples[0])
    beam_partial = jnp.stack([beam_real, beam_imag])
    beams_dev = BEAMS // elem_count
    beam_all = lax.psum(beam_partial, "elem")
    own_beams = lax.dynamic_slice_in_dim(beam_all, lax.axis_index("elem") * beams_dev, beams_dev, 1)
    earlier = from_behind(own_beams, "tm", 1)
    frames = span_len // CHANNELS
    extended = jnp.concatenate([earlier, own_beams], 2).reshape(
        2, beams_dev, TAPS - 1 + frames, CHANNELS
    )
    taps = tap_table.astype(jnp.float32) / 2048.0
    folded = jnp.zeros((2, beams_dev, frames, CHANNELS), jnp.float32)
    for tap in range(TAPS):
        folded = folded + taps[tap] * extended[:, :, TAPS - 1 - tap : TAPS - 1 - tap + frames, :]
    channel_ids = lax.iota(jnp.int32, CHANNELS)
    products = channel_ids[:, None] * channel_ids[None, :] % CHANNELS
    angle = 2.0 * math.pi / CHANNELS * products.astype(jnp.float32)
    cos_dft = jnp.cos(angle)
    sin_dft = jnp.sin(angle)
    fold_real = folded[0].reshape(beams_dev * frames, CHANNELS)
    fold_imag = folded[1].reshape(beams_dev * frames, CHANNELS)
    norm_factor = 1.0 / math.sqrt(CHANNELS)
    spec_real = (matmul(fold_real, cos_dft) + matmul(fold_imag, sin_dft)) * norm_factor
    spec_imag = (matmul(fold_imag, cos_dft) - matmul(fold_real, sin_dft)) * norm_factor
    spectra = jnp.stack([spec_real, spec_imag]).reshape(2, beams_dev, frames, CHANNELS)
    return (spectra, vector)


def solution(mesh):
    return jax.shard_map(
        body,
        mesh=mesh,
        in_specs=(P(None, "elem", "tm"), P(), P(None, "elem", None), P()),
        out_specs=(P(None, "elem", "tm", None), P(None, "elem", None)),
        check_vma=False,
    )
```

profile of v0, /device:TPU:4, one launch (start us, length us, event | category | flops | bytes accessed | tf_op | source)
XLA Modules:
  0.0 614.1 jit_solution(17744367124881341390)
XLA Ops:
  7.2 5.8 copy.13
  12.9 4.9 all-to-all-start
  18.5 70.0 %all-to-all-done = f32[2,128,3072]{1,0,2:T(2,128)S(1)} async-done(((f32[2,128,3072]{1,0,2:T(2,128)}), f32[2,128,3072]{1,0,2:T(2,128)S(1)}, u32[]{:S(2)}, u32[]{:S(2)}) %all-to-all-start) | async-done | bytes 3145760 | tf_op jit(solution)/shard_map/all_to_all | solution.py:97
  90.5 1.9 copy.16
  92.7 22.0 %fusion = f32[2048,1024]{1,0:T(8,128)S(1)} fusion(f32[512,768]{1,0:T(8,128)S(1)} %get-tuple-element.13, f32[512,768]{1,0:T(8,128)S(1)} %get-tuple-element.12, f32[512,768]{1,0:T(8,128)S(1)} %bitcast.215, f32[512,768]{1,0:T(8,128)S(1)} %bitcast.214), kind=kOutput, calls=%fused_computation | convolution fusion | flops 19332857856 | bytes 14680064 | tf_op jit(solution)/shard_map/dot_general | solution.py:39
  115.8 12.2 %pad_maximum_fusion = f32[4,512,512]{2,1,0:T(8,128)} fusion(f32[1,512,512]{2,1,0:T(8,128)S(1)} %get-tuple-element.11, f32[1,512,512]{2,1,0:T(8,128)S(1)} %get-tuple-element.10, f32[1,512,512]{2,1,0:T(8,128)S(1)} %get-tuple-element.9, f32[1,512,512]{2,1,0:T(8,128)S(1)} %get-tuple-element.8), kind=kLoop, calls=%fused_computation.14 | loop fusion | flops 3145728 | bytes 8388608 | tf_op jit(solution)/shard_map/stack | solution.py:73
  128.1 76.0 %reduce-scatter.2.cloned.1.call-done = f32[4,128,512]{2,1,0:T(8,128)} async-done(((f32[4,512,512]{2,1,0:T(8,128)}), f32[4,128,512]{2,1,0:T(8,128)}) %reduce-scatter.2.cloned.1.call-update) | async-done | bytes 1048592 | tf_op jit(solution)/shard_map/reduce_scatter | solution.py:104
  204.2 11.2 %psum.64 = f32[64]{0:T(128)S(1)} all-reduce(f32[64]{0:T(128)S(1)} %multiply_reduce_fusion.3), channel_id=1, replica_groups=mesh['tm'=8,'elem'=4] {'elem'}, use_global_device_ids=true, to_apply=%region_3.4 | all-reduce | flops 64 | bytes 512 | tf_op jit(solution)/shard_map/psum | solution.py:88
  215.5 48.0 %all-reduce.6.cloned.1.call-done = f32[4,128,512]{2,1,0:T(8,128)} async-done(((f32[4,128,512]{2,1,0:T(8,128)}), f32[4,128,512]{2,1,0:T(8,128)}) %all-reduce.6.cloned.1.call-update) | async-done | bytes 1048592 | tf_op jit(solution)/shard_map/psum | solution.py:105
  274.7 38.8 %all-reduce.8.cloned.1.call-done = f32[4,512,64]{1,2,0:T(8,128)} async-done(((f32[4,512,64]{1,2,0:T(8,128)}), f32[4,512,64]{1,2,0:T(8,128)}) %all-reduce.8.cloned.1.call-update) | async-done | bytes 524304 | tf_op jit(solution)/shard_map/psum | solution.py:125
  319.7 10.6 %psum.66 = f32[64]{0:T(128)S(1)} all-reduce(f32[64]{0:T(128)S(1)} %multiply_reduce_fusion.2), channel_id=1, replica_groups=mesh['tm'=8,'elem'=4] {'elem'}, use_global_device_ids=true, to_apply=%region_6.7 | all-reduce | flops 64 | bytes 512 | tf_op jit(solution)/shard_map/psum | solution.py:88
  333.9 36.9 %all-reduce.10.cloned.1.call-done = f32[4,512,64]{1,2,0:T(8,128)} async-done(((f32[4,512,64]{1,2,0:T(8,128)}), f32[4,512,64]{1,2,0:T(8,128)}) %all-reduce.10.cloned.1.call-update) | async-done | bytes 524304 | tf_op jit(solution)/shard_map/psum | solution.py:125
  377.1 10.6 %psum.68 = f32[64]{0:T(128)S(1)} all-reduce(f32[64]{0:T(128)S(1)} %multiply_reduce_fusion.1), channel_id=1, replica_groups=mesh['tm'=8,'elem'=4] {'elem'}, use_global_device_ids=true, to_apply=%region_9.10 | all-reduce | flops 64 | bytes 512 | tf_op jit(solution)/shard_map/psum | solution.py:88
  391.2 36.9 %all-reduce.12.cloned.1.call-done = f32[4,512,64]{1,2,0:T(8,128)} async-done(((f32[4,512,64]{1,2,0:T(8,128)}), f32[4,512,64]{1,2,0:T(8,128)}) %all-reduce.12.cloned.1.call-update) | async-done | bytes 524304 | tf_op jit(solution)/shard_map/psum | solution.py:125
  434.4 10.9 %psum.70 = f32[64]{0:T(128)S(1)} all-reduce(f32[64]{0:T(128)S(1)} %multiply_reduce_fusion), channel_id=1, replica_groups=mesh['tm'=8,'elem'=4] {'elem'}, use_global_device_ids=true, to_apply=%region_12.13 | all-reduce | flops 64 | bytes 512 | tf_op jit(solution)/shard_map/psum | solution.py:88
  445.4 2.4 fusion.33
  447.8 2.4 fusion.29
  453.4 67.3 %all-reduce.14.cloned.1.call-done = f32[2,64,3072]{2,1,0:T(8,128)} async-done(((f32[2,64,3072]{2,1,0:T(8,128)}), f32[2,64,3072]{2,1,0:T(8,128)}) %all-reduce.14.cloned.1.call-update) | async-done | bytes 1572880 | tf_op jit(solution)/shard_map/psum | solution.py:136
  521.7 2.1 collective-permute-start
  523.9 7.8 %collective-permute-done = f32[2,16,3072]{2,1,0:T(8,128)S(1)} collective-permute-done((f32[2,16,3072]{2,1,0:T(8,128)S(1)}, f32[2,16,3072]{2,1,0:T(8,128)S(1)}, u32[]{:S(2)}, u32[]{:S(2)}) %collective-permute-start) | collective-permute-done | bytes 393248 | tf_op jit(solution)/shard_map/ppermute | solution.py:22
  532.8 18.0 %fusion.23 = f32[48,1024]{1,0:T(8,128)S(1)} fusion(f32[48,1024]{1,0:T(8,128)S(1)} %reshape_squeeze.6), kind=kOutput, calls=%fused_computation.28 | convolution fusion | flops 618659840 | bytes 393216 | tf_op jit(solution)/shard_map/dot_general | solution.py:59
  550.9 18.0 %fusion.21 = f32[48,1024]{1,0:T(8,128)S(1)} fusion(f32[48,1024]{1,0:T(8,128)S(1)} %reshape_squeeze.7), kind=kOutput, calls=%fused_computation.27 | convolution fusion | flops 618659840 | bytes 393216 | tf_op jit(solution)/shard_map/dot_general | solution.py:59
  569.0 18.4 %fusion.42 = f32[48,1024]{1,0:T(8,128)S(1)} fusion(f32[48,1024]{1,0:T(8,128)S(1)} %fusion.23, f32[48,1024]{1,0:T(8,128)S(1)} %reshape_squeeze.7), kind=kOutput, calls=%fused_computation.45 | convolution fusion | flops 618758144 | bytes 589824 | tf_op jit(solution)/shard_map/dot_general | solution.py:59
  587.4 18.1 %fusion.48 = f32[48,1024]{1,0:T(8,128)S(1)} fusion(f32[48,1024]{1,0:T(8,128)S(1)} %fusion.21, f32[48,1024]{1,0:T(8,128)S(1)} %reshape_squeeze.6), kind=kOutput, calls=%fused_computation.47 | convolution fusion | flops 618758144 | bytes 589824 | tf_op jit(solution)/shard_map/dot_general | solution.py:59
  (98 shorter events, 47.3 us)
Async XLA Ops:
  12.9 75.5 %all-to-all-start = ((f32[2,128,3072]{1,0,2:T(2,128)}), f32[2,128,3072]{1,0,2:T(2,128)S(1)}, u32[]{:S(2)}, u32[]{:S(2)}) async-start(f32[2,128,3072]{1,0,2:T(2,128)} %copy.13), calls=%async_computation | async-start | bytes 6291456 | tf_op jit(solution)/shard_map/all_to_all | solution.py:97
  17.8 186.2 %reduce-scatter.2.cloned.1.call-start = ((), (), s32[]{:S(2)}) async-start(), calls=%async_computation.2 | async-start | bytes 5242880 | tf_op jit(solution)/shard_map/reduce_scatter | solution.py:104
  128.0 76.1 %copy-start.3 = (s32[2,128,64]{1,2,0:T(8,128)S(1)}, s32[2,128,64]{1,2,0:T(8,128)}, u32[]{:S(2)}) copy-start(s32[2,128,64]{1,2,0:T(8,128)} %param.6) | copy-start | bytes 196612
  128.0 135.5 %all-reduce.6.cloned.1.call-start = ((), (), s32[]{:S(2)}) async-start(), calls=%async_computation.3 | async-start | bytes 2097152 | tf_op jit(solution)/shard_map/psum | solution.py:105
  204.0 109.4 %all-reduce.8.cloned.1.call-start = ((), (), s32[]{:S(2)}) async-start(), calls=%async_computation.4 | async-start | bytes 1048576 | tf_op jit(solution)/shard_map/psum | solution.py:125
  263.6 49.9 %copy-start = (f32[4,128,512]{2,1,0:T(8,128)S(1)}, f32[4,128,512]{2,1,0:T(8,128)}, u32[]{:S(2)}) copy-start(f32[4,128,512]{2,1,0:T(8,128)} %all-reduce.6.cloned.1.call-done) | copy-start | bytes 3145732
  274.6 96.2 %all-reduce.10.cloned.1.call-start = ((), (), s32[]{:S(2)}) async-start(), calls=%async_computation.5 | async-start | bytes 1048576 | tf_op jit(solution)/shard_map/psum | solution.py:125
  333.8 94.3 %all-reduce.12.cloned.1.call-start = ((), (), s32[]{:S(2)}) async-start(), calls=%async_computation.6 | async-start | bytes 1048576 | tf_op jit(solution)/shard_map/psum | solution.py:125
  391.2 129.5 %all-reduce.14.cloned.1.call-start = ((), (), s32[]{:S(2)}) async-start(), calls=%async_computation.7 | async-start | bytes 3145728 | tf_op jit(solution)/shard_map/psum | solution.py:136
  434.3 15.8 %copy-start.1 = (f32[2,128,3072]{2,1,0:T(8,128)S(1)}, f32[2,128,3072]{2,1,0:T(8,128)}, u32[]{:S(2)}) copy-start(f32[2,128,3072]{2,1,0:T(8,128)} %param.4) | copy-start | bytes 9437188
  445.4 6.7 %copy-start.2 = (f32[2,128,64]{1,2,0:T(8,128)}, f32[2,128,64]{1,2,0:T(8,128)S(1)}, u32[]{:S(2)}) copy-start(f32[2,128,64]{1,2,0:T(8,128)S(1)} %fusion.111) | copy-start | bytes 196612
  451.1 72.7 %copy-start.4 = (s32[4,1024]{1,0:T(4,128)S(1)}, s32[4,1024]{1,0:T(4,128)}, u32[]{:S(2)}) copy-start(s32[4,1024]{1,0:T(4,128)} %param.7) | copy-start | bytes 49156
  521.7 10.0 %collective-permute-start = (f32[2,16,3072]{2,1,0:T(8,128)S(1)}, f32[2,16,3072]{2,1,0:T(8,128)S(1)}, u32[]{:S(2)}, u32[]{:S(2)}) collective-permute-start(f32[2,16,3072]{2,1,0:T(8,128)S(1)} %constant_dynamic-slice_fusion), channel_id=1, source_target_pairs={{0,4},{4,8},{8,12},{12,16},{16,20},{20,24},{24,28},{1,5},{5,9},{9,... | collective-permute-start | bytes 1179656 | tf_op jit(solution)/shard_map/ppermute | solution.py:22
Sparse Core Ops, SparseCore 0:
  128.1 75.8 reduce-scatter.1
  207.2 56.3 all-reduce.5
  274.7 38.6 all-reduce.7
  333.9 36.8 all-reduce.9
  391.3 36.7 all-reduce.11
  453.5 67.0 all-reduce.13
where the time goes:
time: 624 us; the launch traced here: 614 us
  waiting for transfers between devices  382 us (61%)
  matrix products  132 us (21%)
  blocking collectives  43.3 us (7%)
  other arithmetic  18.8 us (3%)
  between operations  15.7 us (3%)
  local copies, waits for them, and re-layouts  15.5 us (2%)
  starting transfers between devices  7.21 us (1%)
    psum x3, waiting for transfers between devices, body(): lax.psum(jnp.stack([adj_real, adj_imag, herm_real, herm_imag]), 'elem')  113 us
    dot_general x16, matrix products, matmul(): jnp.dot(left_rows, right_rows, precision=HIGH, preferred_element_type=jnp...  88.2 us
    reduce_scatter x1, waiting for transfers between devices, body(): lax.psum_scatter(full_corr, 'elem', scatter_dimension=1, tiled=True)  76 us
    all_to_all x1, waiting for transfers between devices, body(): lax.all_to_all(samples, 'elem', split_axis=2, concat_axis=1, tiled=True)  70 us
    psum x1, waiting for transfers between devices, body(): beam_all = lax.psum(beam_partial, 'elem')  67.3 us
    psum x1, waiting for transfers between devices, body(): summed_corr = lax.psum(partial_corr, 'tm')  48 us
    psum x4, blocking collectives, column_norms(): return lax.psum(column_squares(vector), 'elem')  43.3 us
    dot_general x1, matrix products, contract(): lax.dot_general(left_rows, right_rows, (((1,), (1,)), ((), ())), precisio...  22 us
  transfers between devices with their start and end apart: 8, of which 8 were waited for; matrix products, arithmetic and copies ran while one was open for 0% of the time, Pallas kernels for 0%

commit v1 on v0

v1 whole, which is shorter than its diff:
```python
import math

import jax
import jax.numpy as jnp
from jax import lax
from jax.experimental import pallas as pl
from jax.experimental.pallas import tpu as pltpu
from jax.sharding import PartitionSpec as P

ITERS = 3
EPS = 1e-06
F32 = jnp.float32
BF16 = jnp.bfloat16
NT = (((1,), (1,)), ((), ()))
NN = (((1,), (0,)), ((), ()))


def shifted(x, axis, by):
    devices = lax.axis_size(axis)
    return lax.ppermute(x, axis, [(i, (i + by) % devices) for i in range(devices)])


def swapped(x, axis, bit):
    devices = lax.axis_size(axis)
    return lax.ppermute(x, axis, [(i, i ^ (1 << bit)) for i in range(devices)])


def from_behind(x, axis, by):
    devices = lax.axis_size(axis)
    pairs = [(i, i + by) for i in range(devices) if 0 <= i + by < devices]
    return lax.ppermute(x, axis, pairs)


def halves(x, flag):
    count = x.shape[0] // 2
    keep = lax.dynamic_slice_in_dim(x, flag * count, count, 0)
    send = lax.dynamic_slice_in_dim(x, (1 - flag) * count, count, 0)
    return keep, send


def bit_of(index, bit):
    return (index >> bit) & 1


def joined(own, other, flag):
    return jnp.where(
        flag == 0, jnp.concatenate([own, other], 0), jnp.concatenate([other, own], 0)
    )


def scatter_step(x, axis, bit):
    keep, send = halves(x, bit_of(lax.axis_index(axis), bit))
    return keep + swapped(send, axis, bit)


def gather_step(x, axis, bit):
    return joined(x, swapped(x, axis, bit), bit_of(lax.axis_index(axis), bit))


def summed_everywhere(x):
    tm_bits = list(range(int(math.log2(lax.axis_size("tm")))))
    elem_bits = list(range(int(math.log2(lax.axis_size("elem")))))
    first, rest = tm_bits[:1], tm_bits[1:]
    orders = (rest, rest[::-1])
    for bit in first:
        x = scatter_step(x, "tm", bit)
    half = x.shape[0] // 2
    parts = [x[:half], x[half:]]
    for step in range(len(rest)):
        parts = [scatter_step(part, "tm", order[step]) for part, order in zip(parts, orders)]
    flag = bit_of(lax.axis_index("elem"), 0)
    keep = jnp.where(flag == 0, parts[0], parts[1])
    send = jnp.where(flag == 0, parts[1], parts[0])
    x = keep + swapped(send, "elem", 0)
    for bit in elem_bits[1:]:
        x = scatter_step(x, "elem", bit)
    for bit in elem_bits[:0:-1]:
        x = gather_step(x, "elem", bit)
    other = swapped(x, "elem", 0)
    parts = [jnp.where(flag == 0, x, other), jnp.where(flag == 0, other, x)]
    for step in range(len(rest) - 1, -1, -1):
        parts = [gather_step(part, "tm", order[step]) for part, order in zip(parts, orders)]
    x = jnp.concatenate(parts, 0)
    for bit in first:
        x = gather_step(x, "tm", bit)
    return x


def split(x):
    high = x.astype(BF16)
    return high, (x - high.astype(F32)).astype(BF16)


def split_kept(x):
    high = lax.reduce_precision(x, 8, 7)
    return high.astype(BF16), (x - high).astype(BF16)


def dot(left, right, dims):
    return lax.dot_general(left, right, dims, preferred_element_type=F32)


def triple(left, right, dims):
    return (
        dot(left[0], right[0], dims) + dot(left[0], right[1], dims) + dot(left[1], right[0], dims)
    )


def gram_kernel(has_acc, place_ref, *refs):
    pieces = refs[:4]
    cs_ref = refs[4]
    if has_acc:
        acc_ref = refs[5]
        refs = refs[6:]
    else:
        acc_ref = None
        refs = refs[5:]
    out_ref, lefts = refs[0], refs[1:]
    n = pieces[0].shape[1]
    count = pieces[0].shape[2]
    elems = n * len(pieces)
    for k, piece in enumerate(pieces):
        rows = pl.ds(pl.multiple_of(place_ref[k] * n, n), n)
        real, imag = piece[0], piece[1]
        cosine, sine = cs_ref[0:1, :], cs_ref[1:2, :]
        mod_real = real * cosine + imag * sine
        mod_imag = imag * cosine - real * sine
        real, imag, mod_real, mod_imag = split(real), split(imag), split(mod_real), split(mod_imag)
        for part in range(2):
            for where, (a, b) in enumerate(
                (
                    (real[part], imag[part]),
                    (mod_real[part], mod_imag[part]),
                    (mod_imag[part], -mod_real[part]),
                    (imag[part], -real[part]),
                )
            ):
                ref = lefts[2 * where + part]
                ref[rows, 0:count] = a
                ref[rows, count:] = b

    def product(where, top, height, left, width):
        a = tuple(lefts[2 * where + part][pl.ds(top, height), :] for part in range(2))
        b = tuple(lefts[part][pl.ds(left, width), :] for part in range(2))
        return triple(a, b, NT)

    def put(top, height, left, width, value):
        if acc_ref is not None:
            value = value + acc_ref[pl.ds(top, height), pl.ds(left, width)]
        out_ref[pl.ds(top, height), pl.ds(left, width)] = value

    half = elems // 2
    for top in (0, half):
        put(top, half, 0, elems, product(1, top, half, 0, elems))
        put(elems + top, half, 0, elems, product(2, top, half, 0, elems))
    base = 2 * elems
    put(base, half, half, half, product(0, 0, half, half, half))
    put(base + half, half, 0, half, product(3, half, half, 0, half))
    above = lax.broadcasted_iota(jnp.int32, (half, half), 0) <= lax.broadcasted_iota(
        jnp.int32, (half, half), 1
    )
    for top in (0, half):
        both = jnp.where(
            above, product(0, top, half, top, half), product(3, top, half, top, half)
        )
        put(base + top, half, top, half, both)


def gram(place, pieces, cs, acc):
    elems = pieces[0].shape[1] * len(pieces)
    count = pieces[0].shape[2]
    vmem = pl.BlockSpec(memory_space=pltpu.VMEM)
    args = [place, *pieces, cs] + ([] if acc is None else [acc])
    return pl.pallas_call(
        lambda *refs: gram_kernel(acc is not None, *refs),
        out_shape=jax.ShapeDtypeStruct((3 * elems, elems), F32),
        in_specs=[pl.BlockSpec(memory_space=pltpu.SMEM)] + [vmem] * (len(args) - 1),
        out_specs=vmem,
        scratch_shapes=[pltpu.VMEM((elems, 2 * count), BF16)] * 8,
        input_output_aliases={} if acc is None else {len(args) - 1: 0},
        cost_estimate=pl.CostEstimate(
            flops=2 * 21 * elems * elems * count, bytes_accessed=16 * elems * elems, transcendentals=0
        ),
        name="gram",
    )(*args)


def power_kernel(total, place_ref, corr_ref, *refs):
    starts = refs[:4]
    out_ref = refs[4]
    cr, ci, pr, pi, v_ref = refs[5:7], refs[7:9], refs[9:11], refs[11:13], refs[13]
    elems = corr_ref.shape[1]
    n = starts[0].shape[1]
    rows = starts[0].shape[0]
    beams = rows // 2
    scale = 1.0 / math.sqrt(total * elems)

    def store(pair, value):
        pair[0][...], pair[1][...] = split(value)

    store(cr, corr_ref[0:elems, :] * scale)
    store(ci, corr_ref[elems : 2 * elems, :] * scale)
    packed = corr_ref[2 * elems :, :] * (1.0 / total)
    mirrored = packed.T
    row = lax.broadcasted_iota(jnp.int32, (elems, elems), 0)
    col = lax.broadcasted_iota(jnp.int32, (elems, elems), 1)
    store(pr, jnp.where(row <= col, packed, mirrored))
    store(pi, jnp.where(row > col, packed, jnp.where(row < col, -mirrored, 0.0)))
    for k, start in enumerate(starts):
        v_ref[:, pl.ds(pl.multiple_of(place_ref[k] * n, n), n)] = start[...] - 4.5

    def normalized(v):
        squares = jnp.sum(v * v, axis=1, keepdims=True)
        squares = squares[:beams] + squares[beams:]
        inverse = 1.0 / jnp.sqrt(squares + EPS)
        return v * jnp.concatenate([inverse, inverse], 0)

    def times(v, pair, dims):
        high, low = split(v)
        both = dot(jnp.concatenate([high, low], 0), pair[0][...], dims)
        return both[:rows] + both[rows:] + dot(high, pair[1][...], dims)

    v = normalized(v_ref[...])
    for _ in range(ITERS):
        by_real = times(v, cr, NN)
        by_imag = times(v, ci, NN)
        w = jnp.concatenate(
            [by_real[:beams] + by_imag[beams:], by_real[beams:] - by_imag[:beams]], 0
        )
        by_real = times(w, cr, NT) + times(v, pr, NT)
        by_imag = times(w, ci, NT) + times(v, pi, NT)
        v = normalized(
            jnp.concatenate(
                [by_real[:beams] - by_imag[beams:], by_real[beams:] + by_imag[:beams]], 0
            )
        )
    out_ref[...] = v


def power(total, place, corr, starts):
    elems = corr.shape[1]
    rows = starts[0].shape[0]
    vmem = pl.BlockSpec(memory_space=pltpu.VMEM)
    return pl.pallas_call(
        lambda *refs: power_kernel(total, *refs),
        out_shape=jax.ShapeDtypeStruct((rows, elems), F32),
        in_specs=[pl.BlockSpec(memory_space=pltpu.SMEM)] + [vmem] * (1 + len(starts)),
        out_specs=vmem,
        scratch_shapes=[pltpu.VMEM((elems, elems), BF16)] * 8 + [pltpu.VMEM((rows, elems), F32)],
        cost_estimate=pl.CostEstimate(
            flops=ITERS * 36 * elems * elems * rows, bytes_accessed=16 * elems * elems, transcendentals=0
        ),
        name="power",
    )(place, corr, *starts)


def beam_kernel(place_ref, v_ref, *refs):
    pieces, out_ref = refs[:-1], refs[-1]
    rows = v_ref.shape[0]
    beams = rows // 2
    n = pieces[0].shape[1]
    count = pieces[0].shape[2]
    lefts = []
    for k in range(4):
        v = v_ref[:, pl.ds(pl.multiple_of(place_ref[k] * n, n), n)]
        high, low = split(v)
        lefts.append((jnp.concatenate([high, low], 0), high))
    for chunk in range(len(pieces) // 4):
        totals = []
        for half in range(2):
            total = 0.0
            for k in range(4):
                high, low = split(pieces[4 * chunk + k][half])
                both = dot(lefts[k][0], high, NN)
                total = total + (both[:rows] + both[rows:] + dot(lefts[k][1], low, NN))
            totals.append(total)
        by_real, by_imag = totals
        cols = pl.ds(chunk * count, count)
        out_ref[0, :, cols] = by_real[:beams] + by_imag[beams:]
        out_ref[1, :, cols] = by_imag[:beams] - by_real[beams:]


def beams_of(place, v, pieces):
    beams = v.shape[0] // 2
    count = pieces[0].shape[2] * (len(pieces) // 4)
    vmem = pl.BlockSpec(memory_space=pltpu.VMEM)
    return pl.pallas_call(
        beam_kernel,
        out_shape=jax.ShapeDtypeStruct((2, beams, count), F32),
        in_specs=[pl.BlockSpec(memory_space=pltpu.SMEM)] + [vmem] * (1 + len(pieces)),
        out_specs=vmem,
        name="beams",
    )(place, v, *pieces)


def dft_kernel(place_ref, *refs):
    pieces = refs[:4]
    ch, cl, sh, sl, out_ref = refs[4:]
    rows = pieces[0].shape[1]
    count = pieces[0].shape[2]
    by_cos, by_sin = 0.0, 0.0
    for k, piece in enumerate(pieces):
        where = pl.ds(pl.multiple_of(place_ref[k] * count, count), count)
        high, low = split(jnp.concatenate([piece[0], piece[1]], 0))
        both = jnp.concatenate([high, low], 0)
        for table in range(2):
            t_high, t_low = ((ch, cl), (sh, sl))[table]
            value = dot(both, t_high[where, :], NN)
            value = value[: 2 * rows] + value[2 * rows :] + dot(high, t_low[where, :], NN)
            if table == 0:
                by_cos = by_cos + value
            else:
                by_sin = by_sin + value
    out_ref[0] = by_cos[:rows] + by_sin[rows:]
    out_ref[1] = by_cos[rows:] - by_sin[:rows]


def dft(place, pieces, tables):
    rows = pieces[0].shape[1]
    channels = tables[0].shape[0]
    width = 256
    whole = pl.BlockSpec(pieces[0].shape, lambda i: (0, 0, 0))
    return pl.pallas_call(
        dft_kernel,
        grid=(channels // width,),
        out_shape=jax.ShapeDtypeStruct((2, rows, channels), F32),
        in_specs=[pl.BlockSpec(memory_space=pltpu.SMEM)]
        + [whole] * 4
        + [pl.BlockSpec((channels, width), lambda i: (0, i))] * 4,
        out_specs=pl.BlockSpec((2, rows, width), lambda i: (0, 0, i)),
        name="dft",
    )(place, *pieces, *tables)


def rotation(shift_bin, times, modulus):
    folded = shift_bin[0] * times % modulus
    angle = 2.0 * math.pi / modulus * folded.astype(F32)
    return jnp.stack([jnp.cos(angle), jnp.sin(angle)])


def dft_tables(channels):
    step = 32
    f = lax.iota(jnp.int32, channels)[None, :]

    def rows(count, factor):
        k = factor * lax.iota(jnp.int32, count)[:, None] * f % channels
        angle = 2.0 * math.pi / channels * k.astype(F32)
        return jnp.cos(angle), jnp.sin(angle)

    coarse, fine = rows(channels // step, step), rows(step, 1)
    a_cos, a_sin = (t[:, None, :] for t in coarse)
    b_cos, b_sin = (t[None, :, :] for t in fine)
    norm = 1.0 / math.sqrt(channels)
    cosine = ((a_cos * b_cos - a_sin * b_sin) * norm).reshape(channels, channels)
    sine = ((a_sin * b_cos + a_cos * b_sin) * norm).reshape(channels, channels)
    return (*split_kept(cosine), *split_kept(sine))


def body(samples, shift_bin, start_vectors, tap_table):
    taps_count, channels = tap_table.shape
    span_len = samples.shape[2]
    devices = lax.axis_size("elem")
    modulus = span_len * lax.axis_size("tm")
    frames = span_len // channels
    quarter = channels // devices
    mine = lax.axis_index("elem")
    span_start = lax.axis_index("tm") * span_len
    place = jnp.stack([(mine - k) % devices for k in range(devices)])

    own_start = start_vectors.astype(F32).transpose(0, 2, 1).reshape(-1, start_vectors.shape[1])
    starts = [own_start] + [shifted(own_start, "elem", k) for k in range(1, devices)]

    chunks = []
    corr = None
    for frame in range(frames):
        own = []
        for k in range(devices):
            begin = frame * channels + (mine + k) % devices * quarter
            own.append(lax.dynamic_slice_in_dim(samples, begin, quarter, 2))
        if frame >= 2:
            own[1:], _ = lax.optimization_barrier((own[1:], chunks[frame - 2]))
        pieces = [own[0]] + [shifted(own[k], "elem", k) for k in range(1, devices)]
        times = span_start + frame * channels + mine * quarter + lax.iota(jnp.int32, quarter)
        rotated = rotation(shift_bin, times, modulus)
        if frame == 0:
            tables = dft_tables(channels)
            rotated, tables = lax.optimization_barrier((rotated, tables))
        corr = gram(place, pieces, rotated, corr)
        chunks.append(pieces)

    corr = summed_everywhere(corr)
    v = power(modulus, place, corr, starts)
    beams = v.shape[0] // 2
    elems_dev = samples.shape[1]
    weights = (
        lax.dynamic_slice_in_dim(v, mine * elems_dev, elems_dev, 1)
        .reshape(2, beams, elems_dev)
        .transpose(0, 2, 1)
    )
    b = beams_of(place, v, [piece for pieces in chunks for piece in pieces])
    extended = jnp.concatenate([from_behind(b[:, :, -(taps_count - 1) * quarter :], "tm", 1), b], 2)
    taps = lax.dynamic_slice_in_dim(tap_table, mine * quarter, quarter, 1).astype(F32) / 2048.0
    folded = []
    for frame in range(frames):
        w = 0.0
        for tap in range(taps_count):
            at = taps_count - 1 + frame - tap
            w = w + taps[tap] * extended[:, :, at * quarter : (at + 1) * quarter]
        folded.append(w)
    folded = jnp.stack(folded, 1)
    beams_dev = beams // devices
    received = []
    for k in range(devices):
        part = lax.dynamic_slice_in_dim(folded, (mine + k) % devices * beams_dev, beams_dev, 2)
        part = part.reshape(2, frames * beams_dev, quarter)
        received.append(part if k == 0 else shifted(part, "elem", k))
    spectra = dft(place, received, tables)
    spectra = spectra.reshape(2, frames, beams_dev, channels).transpose(0, 2, 1, 3)
    return (spectra, weights.reshape(2, elems_dev, beams))


def solution(mesh):
    return jax.shard_map(
        body,
        mesh=mesh,
        in_specs=(P(None, "elem", "tm"), P(), P(None, "elem", None), P()),
        out_specs=(P(None, "elem", "tm", None), P(None, "elem", None)),
        check_vma=False,
    )
```

time: 624 us -> 204 us (0.33); the launches traced: 614 us -> 203 us
  waiting for transfers between devices: 382 us -> 78.8 us
  matrix products: 132 us -> 0 us
  starting transfers between devices: 7.21 us -> 52.1 us
  blocking collectives: 43.3 us -> 0 us
  Pallas kernels: 0 us -> 40.4 us
  between operations: 15.7 us -> 1.73 us
    psum x5 -> x0, waiting for transfers between devices: 228 us -> none  [the longest x3 113 us: body(): lax.psum(jnp.stack([adj_real, adj_imag, herm_real, herm_imag]), 'elem')]
    dot_general x45 -> x0, matrix products: 132 us -> none  [the longest x16 88.2 us: matmul(): jnp.dot(left_rows, right_rows, precision=HIGH, preferred_element_type=jnp...]
    reduce_scatter x1 -> x0, waiting for transfers between devices: 76 us -> none  [body(): lax.psum_scatter(full_corr, 'elem', scatter_dimension=1, tiled=True)]
    ppermute x0 -> x29, waiting for transfers between devices: none -> 71.3 us  [the longest x14 46.3 us: swapped(): return lax.ppermute(x, axis, [(i, i ^ 1 << bit) for i in range(devices)])]
    all_to_all x1 -> x0, waiting for transfers between devices: 70 us -> none  [body(): lax.all_to_all(samples, 'elem', split_axis=2, concat_axis=1, tiled=True)]
    ppermute x0 -> x29, starting transfers between devices: none -> 50.2 us  [the longest x15 28.9 us: shifted(): lax.ppermute(x, axis, [(i, (i + by) % devices) for i in range(devices)])]
    psum x4 -> x0, blocking collectives: 43.3 us -> none  [column_norms(): return lax.psum(column_squares(vector), 'elem')]
    pallas_call x0 -> x6, Pallas kernels: none -> 40.4 us  [the longest x3 21.3 us: gram(): pl.pallas_call(lambda *refs: gram_kernel(acc is not None, *refs), out_sha...]
  transfers between devices with their start and end apart: 8 -> 30, of which waited for: 8 -> 19; matrix products, arithmetic and copies ran while one was open for 0% -> 9% of each run, Pallas kernels for 0% -> 7%
where the time goes in v1:
time: 204 us; the launch traced here: 203 us
  waiting for transfers between devices  78.8 us (39%)
  starting transfers between devices  52.1 us (26%)
  Pallas kernels  40.4 us (20%)
  other arithmetic  18.7 us (9%)
  local copies, waits for them, and re-layouts  11.6 us (6%)
    ppermute x14, waiting for transfers between devices, swapped(): return lax.ppermute(x, axis, [(i, i ^ 1 << bit) for i in range(devices)])  46.3 us
    ppermute x15, starting transfers between devices, shifted(): lax.ppermute(x, axis, [(i, (i + by) % devices) for i in range(devices)])  28.9 us
    ppermute x15, waiting for transfers between devices, shifted(): lax.ppermute(x, axis, [(i, (i + by) % devices) for i in range(devices)])  25 us
    ppermute x14, starting transfers between devices, swapped(): return lax.ppermute(x, axis, [(i, i ^ 1 << bit) for i in range(devices)])  21.3 us
    pallas_call x3, Pallas kernels, gram(): pl.pallas_call(lambda *refs: gram_kernel(acc is not None, *refs), out_sha...  21.3 us
    pallas_call x1, Pallas kernels, power(): pl.pallas_call(lambda *refs: power_kernel(total, *refs), out_shape=jax.Sh...  9.12 us
    ppermute x1, waiting for transfers between devices, from_behind(): return lax.ppermute(x, axis, pairs)  7.54 us
    pallas_call x1, Pallas kernels, dft(): pl.pallas_call(dft_kernel, grid=(channels // width,), out_shape=jax.Shape...  5.94 us
  transfers between devices with their start and end apart: 30, of which 19 were waited for; matrix products, arithmetic and copies ran while one was open for 9% of the time, Pallas kernels for 7%

profile of v1, /device:TPU:4, one launch (start us, length us, event | category | flops | bytes accessed | tf_op | source)
XLA Modules:
  0.0 203.4 jit_solution(15256389093313953025)
XLA Ops:
  0.7 3.1 %constant_dynamic-slice_fusion.11 = (f32[2,128,256]{2,1,0:T(8,128)S(1)}, f32[2,128,256]{2,1,0:T(8,128)}, f32[2,128,256]{2,1,0:T(8,128)}, f32[2,128,256]{2,1,0:T(...) fusion(f32[2,128,3072]{2,1,0:T(8,128)} %param.4, ...), kind=kLoop, calls=%fused_computation.68 | loop fusion | bytes 6291504 | tf_op jit(solution)/shard_map/dynamic_slice | solution.py:379
  14.4 5.1 %fusion = (bf16[1024,1024]{1,0:T(8,128)(2,1)}, bf16[1024,1024]{1,0:T(8,128)(2,1)}, bf16[1024,1024]{1,0:T(8,128)(2,1)}, bf16[1024,1024]{1,0:T(8,128)(2,1)}) fusion(f32[32,32,1024]{2,1,0:T(8,128)S(1)} %get-tuple-element.40, f32[32,32,1024]{2,1,0:T(8,128)S(1)} %get-tuple-element.39), kind=kLoop, calls=%fused_computation.4 | loop fusion | flops 8388608 | bytes 16777216 | tf_op jit(solution)/shard_map/convert_element_type | solution.py:96
  24.3 11.4 %collective-permute-done.1.refs_3_.refs_2_ = f32[2,128,256]{2,1,0:T(8,128)S(1)} collective-permute-done((f32[2,128,256]{2,1,0:T(8,128)}, f32[2,128,256]{2,1,0:T(8,128)S(1)}, u32[]{:S(2)}, u32[]{:S(2)}) %collective-permute-start.1) | collective-permute-done | bytes 262176 | tf_op jit(solution)/shard_map/ppermute | solution.py:20
  35.7 8.2 %collective-permute-start.3 = (f32[2,128,256]{2,1,0:T(8,128)S(1)}, f32[2,128,256]{2,1,0:T(8,128)S(1)}, u32[]{:S(2)}, u32[]{:S(2)}) collective-permute-start(f32[2,128,256]{2,1,0:T(8,128)S(1)} %get-tuple-element.10), channel_id=1, source_target_pairs={{0,1},{1,2},{2,3},{3,0},{4,5},{5,6},{6,7},{7,4},{8,9},{9,10},{10,1... | collective-permute-start | bytes 786440 | tf_op jit(solution)/shard_map/ppermute | solution.py:20
  45.5 6.4 %gram.3.refs_6_ = f32[1536,512]{1,0:T(8,128)} custom-call(s32[4]{0:T(128)} %pad_add_fusion.refs_0_.place_ref, f32[2,128,256]{2,1,0:T(8,128)} %get-tuple-element.28.refs_1_.refs_0_, f32[2,128,256]{2,1,0:T(8,128)} %copy-done.1, f32[2,128,256]{2,1,0:T(8,128)} %copy-done.2, f32[2,128,256]{2,1,0:T(8,128)} %copy-done.3, f32[2,256]{1,0:T(2,128)} %pad_maximum_fusion.4.refs_5_), custom_call_target="tpu_custom_call" | custom-call | flops 2818572288 | bytes 4194304 | tf_op jit(solution)/shard_map/gram/pallas_call | solution.py:174
  52.7 6.5 %collective-permute-done.7.refs_3_.refs_6_ = f32[2,128,256]{2,1,0:T(8,128)S(1)} collective-permute-done((f32[2,128,256]{2,1,0:T(8,128)S(1)}, f32[2,128,256]{2,1,0:T(8,128)S(1)}, u32[]{:S(2)}, u32[]{:S(2)}) %collective-permute-start.7) | collective-permute-done | bytes 262176 | tf_op jit(solution)/shard_map/ppermute | solution.py:20
  59.9 7.4 %gram.4.refs_6_ = f32[1536,512]{1,0:T(8,128)} custom-call(s32[4]{0:T(128)} %pad_add_fusion.refs_0_.place_ref, f32[2,128,256]{2,1,0:T(8,128)} %get-tuple-element.24.refs_1_.refs_4_, f32[2,128,256]{2,1,0:T(8,128)} %copy-done.4, f32[2,128,256]{2,1,0:T(8,128)} %copy-done.5, f32[2,128,256]{2,1,0:T(8,128)} %copy-done.6, ...), custom_call_target="tpu_custom_call", output_to_operand_aliasing={{}: (6, {})} | custom-call | flops 2818572288 | bytes 4194304 | tf_op jit(solution)/shard_map/gram/pallas_call | solution.py:174
  71.2 7.5 %gram.5 = f32[1536,512]{1,0:T(8,128)} custom-call(s32[4]{0:T(128)} %pad_add_fusion.refs_0_.place_ref, f32[2,128,256]{2,1,0:T(8,128)} %get-tuple-element.32.refs_1_.refs_8_, f32[2,128,256]{2,1,0:T(8,128)} %copy-done.7, f32[2,128,256]{2,1,0:T(8,128)} %copy-done.8, f32[2,128,256]{2,1,0:T(8,128)} %copy-done.9, ...), custom_call_target="tpu_custom_call", output_to_operand_aliasing={{}: (6, {})} | custom-call | flops 2818572288 | bytes 4194304 | tf_op jit(solution)/shard_map/gram/pallas_call | solution.py:174
  81.5 3.7 %collective-permute-done.9 = f32[768,512]{1,0:T(8,128)} collective-permute-done((f32[768,512]{1,0:T(8,128)}, f32[768,512]{1,0:T(8,128)}, u32[]{:S(2)}, u32[]{:S(2)}) %collective-permute-start.9) | collective-permute-done | bytes 1572896 | tf_op jit(solution)/shard_map/ppermute | solution.py:25
  89.3 9.1 %collective-permute-done.12 = f32[192,512]{1,0:T(8,128)S(1)} collective-permute-done((f32[192,512]{1,0:T(8,128)S(1)}, f32[192,512]{1,0:T(8,128)S(1)}, u32[]{:S(2)}, u32[]{:S(2)}) %collective-permute-start.12) | collective-permute-done | bytes 393248 | tf_op jit(solution)/shard_map/ppermute | solution.py:25
  100.7 3.9 %collective-permute-done.13 = f32[96,512]{1,0:T(8,128)S(1)} collective-permute-done((f32[96,512]{1,0:T(8,128)S(1)}, f32[96,512]{1,0:T(8,128)S(1)}, u32[]{:S(2)}, u32[]{:S(2)}) %collective-permute-start.13) | collective-permute-done | bytes 196640 | tf_op jit(solution)/shard_map/ppermute | solution.py:25
  106.1 6.1 %collective-permute-start.14 = (f32[96,512]{1,0:T(8,128)S(1)}, f32[96,512]{1,0:T(8,128)S(1)}, u32[]{:S(2)}, u32[]{:S(2)}) collective-permute-start(f32[96,512]{1,0:T(8,128)S(1)} %broadcast_select_fusion.2), channel_id=1, source_target_pairs={{0,1},{1,0},{2,3},{3,2},{4,5},{5,4},{6,7},{7,6},{8,9},{9,8},{10,11... | collective-permute-start | bytes 589832 | tf_op jit(solution)/shard_map/ppermute | solution.py:25
  112.1 3.6 %collective-permute-done.14 = f32[96,512]{1,0:T(8,128)S(1)} collective-permute-done((f32[96,512]{1,0:T(8,128)S(1)}, f32[96,512]{1,0:T(8,128)S(1)}, u32[]{:S(2)}, u32[]{:S(2)}) %collective-permute-start.14) | collective-permute-done | bytes 196640 | tf_op jit(solution)/shard_map/ppermute | solution.py:25
  117.6 4.1 %collective-permute-done.15 = f32[48,512]{1,0:T(8,128)S(1)} collective-permute-done((f32[48,512]{1,0:T(8,128)S(1)}, f32[48,512]{1,0:T(8,128)S(1)}, u32[]{:S(2)}, u32[]{:S(2)}) %collective-permute-start.15) | collective-permute-done | bytes 98336 | tf_op jit(solution)/shard_map/ppermute | solution.py:25
  123.3 4.1 %collective-permute-done.16 = f32[48,512]{1,0:T(8,128)S(1)} collective-permute-done((f32[48,512]{1,0:T(8,128)S(1)}, f32[48,512]{1,0:T(8,128)S(1)}, u32[]{:S(2)}, u32[]{:S(2)}) %collective-permute-start.16) | collective-permute-done | bytes 98336 | tf_op jit(solution)/shard_map/ppermute | solution.py:25
  127.4 4.1 %collective-permute-start.17 = (f32[96,512]{1,0:T(8,128)S(1)}, f32[96,512]{1,0:T(8,128)S(1)}, u32[]{:S(2)}, u32[]{:S(2)}) collective-permute-start(f32[96,512]{1,0:T(8,128)S(1)} %maximum_select_fusion.5), channel_id=1, source_target_pairs={{0,1},{1,0},{2,3},{3,2},{4,5},{5,4},{6,7},{7,6},{8,9},{9,8},{10,11... | collective-permute-start | bytes 589832 | tf_op jit(solution)/shard_map/ppermute | solution.py:25
  131.5 3.6 %collective-permute-done.17 = f32[96,512]{1,0:T(8,128)S(1)} collective-permute-done((f32[96,512]{1,0:T(8,128)S(1)}, f32[96,512]{1,0:T(8,128)S(1)}, u32[]{:S(2)}, u32[]{:S(2)}) %collective-permute-start.17) | collective-permute-done | bytes 196640 | tf_op jit(solution)/shard_map/ppermute | solution.py:25
  136.9 6.1 %collective-permute-done.18 = f32[96,512]{1,0:T(8,128)S(1)} collective-permute-done((f32[96,512]{1,0:T(8,128)S(1)}, f32[96,512]{1,0:T(8,128)S(1)}, u32[]{:S(2)}, u32[]{:S(2)}) %collective-permute-start.18) | collective-permute-done | bytes 196640 | tf_op jit(solution)/shard_map/ppermute | solution.py:25
  144.9 6.0 %collective-permute-done.19 = f32[192,512]{1,0:T(8,128)S(1)} collective-permute-done((f32[192,512]{1,0:T(8,128)S(1)}, f32[192,512]{1,0:T(8,128)S(1)}, u32[]{:S(2)}, u32[]{:S(2)}) %collective-permute-start.19) | collective-permute-done | bytes 393248 | tf_op jit(solution)/shard_map/ppermute | solution.py:25
  156.8 4.1 %maximum_select_fusion.refs_1_ = f32[1536,512]{1,0:T(8,128)} fusion(f32[768,512]{1,0:T(8,128)} %collective-permute-done.22, f32[384,512]{1,0:T(8,128)S(1)} %maximum_select_fusion.2, f32[384,512]{1,0:T(8,128)S(1)} %maximum_select_fusion.1, pred[]{:T(512)S(6)} %eq.48), kind=kLoop, calls=%fused_computation.8 | loop fusion | flops 3932160 | bytes 6291457 | tf_op jit(solution)/shard_map/jit(_where)/select_n | solution.py:46
  162.3 9.1 %power.1.v_ref = f32[128,512]{1,0:T(8,128)} custom-call(s32[4]{0:T(128)} %pad_add_fusion.refs_0_.place_ref, f32[1536,512]{1,0:T(8,128)} %maximum_select_fusion.refs_1_, f32[128,128]{1,0:T(8,128)} %bitcast.45, f32[128,128]{1,0:T(8,128)} %copy-done.15, f32[128,128]{1,0:T(8,128)} %copy-done.16, f32[128,128]{1,0:T(8,128)} %copy-done.17), custom_call_target="tpu_custom_call" | custom-call | flops 3623878656 | bytes 4194304 | tf_op jit(solution)/shard_map/power/pallas_call | solution.py:244
  171.5 4.0 %beams.1 = f32[2,64,768]{2,1,0:T(8,128)} custom-call(s32[4]{0:T(128)} %pad_add_fusion.refs_0_.place_ref, f32[128,512]{1,0:T(8,128)} %power.1.v_ref, f32[2,128,256]{2,1,0:T(8,128)} %get-tuple-element.28.refs_1_.refs_0_, f32[2,128,256]{2,1,0:T(8,128)} %copy-done.1, f32[2,128,256]{2,1,0:T(8,128)} %copy-done.2, f32[2,128,256]{2,1,0:T(8,128)} %copy-done.3, ...), custom_call_target="tpu_custom_call" | custom-call | tf_op jit(solution)/shard_map/beams/pallas_call | solution.py:287
  178.2 7.5 %collective-permute-done.26 = f32[2,64,768]{2,1,0:T(8,128)S(1)} collective-permute-done((f32[2,64,768]{2,1,0:T(8,128)}, f32[2,64,768]{2,1,0:T(8,128)S(1)}, u32[]{:S(2)}, u32[]{:S(2)}) %collective-permute-start.26) | collective-permute-done | bytes 393248 | tf_op jit(solution)/shard_map/ppermute | solution.py:31
  197.4 5.9 %dft.1 = f32[2,48,1024]{2,1,0:T(8,128)} custom-call(s32[4]{0:T(128)} %pad_add_fusion.refs_0_.place_ref, f32[2,48,256]{2,1,0:T(8,128)} %bitcast.37, f32[2,48,256]{2,1,0:T(8,128)} %copy-done.10, f32[2,48,256]{2,1,0:T(8,128)} %copy-done.11, f32[2,48,256]{2,1,0:T(8,128)} %copy-done.12, bf16[1024,1024]{1,0:T(8,128)(2,1)} %get-tuple-element.14.refs_4_, ...), custom_call_target="tpu_custom_call" | custom-call | tf_op jit(solution)/shard_map/dft/pallas_call | solution.py:323
  (124 shorter events, 60.8 us)
Async XLA Ops:
  3.9 17.6 %collective-permute-start = (f32[2,128,256]{2,1,0:T(8,128)}, f32[2,128,256]{2,1,0:T(8,128)S(1)}, u32[]{:S(2)}, u32[]{:S(2)}) collective-permute-start(f32[2,128,256]{2,1,0:T(8,128)} %get-tuple-element.27), channel_id=1, source_target_pairs={{0,1},{1,2},{2,3},{3,0},{4,5},{5,6},{6,7},{7,4},{8,9},{9,10},{10,1... | collective-permute-start | bytes 786440 | tf_op jit(solution)/shard_map/ppermute | solution.py:20
  5.4 30.2 %collective-permute-start.1 = (f32[2,128,256]{2,1,0:T(8,128)}, f32[2,128,256]{2,1,0:T(8,128)S(1)}, u32[]{:S(2)}, u32[]{:S(2)}) collective-permute-start(f32[2,128,256]{2,1,0:T(8,128)} %get-tuple-element.26), channel_id=1, source_target_pairs={{0,2},{1,3},{2,0},{3,1},{4,6},{5,7},{6,4},{7,5},{8,10},{9,11},{10,... | collective-permute-start | bytes 786440 | tf_op jit(solution)/shard_map/ppermute | solution.py:20
  8.0 27.6 %collective-permute-start.2 = (f32[2,128,256]{2,1,0:T(8,128)S(1)}, f32[2,128,256]{2,1,0:T(8,128)S(1)}, u32[]{:S(2)}, u32[]{:S(2)}) collective-permute-start(f32[2,128,256]{2,1,0:T(8,128)S(1)} %get-tuple-element.25), channel_id=1, source_target_pairs={{0,3},{1,0},{2,1},{3,2},{4,7},{5,4},{6,5},{7,6},{8,11},{9,8},{10,9... | collective-permute-start | bytes 786440 | tf_op jit(solution)/shard_map/ppermute | solution.py:20
  9.4 42.5 %collective-permute-start.6 = (f32[2,128,256]{2,1,0:T(8,128)}, f32[2,128,256]{2,1,0:T(8,128)S(1)}, u32[]{:S(2)}, u32[]{:S(2)}) collective-permute-start(f32[2,128,256]{2,1,0:T(8,128)} %get-tuple-element.23), channel_id=1, source_target_pairs={{0,1},{1,2},{2,3},{3,0},{4,5},{5,6},{6,7},{7,4},{8,9},{9,10},{10,1... | collective-permute-start | bytes 786440 | tf_op jit(solution)/shard_map/ppermute | solution.py:20
  10.1 49.1 %collective-permute-start.7 = (f32[2,128,256]{2,1,0:T(8,128)S(1)}, f32[2,128,256]{2,1,0:T(8,128)S(1)}, u32[]{:S(2)}, u32[]{:S(2)}) collective-permute-start(f32[2,128,256]{2,1,0:T(8,128)S(1)} %get-tuple-element.33), channel_id=1, source_target_pairs={{0,2},{1,3},{2,0},{3,1},{4,6},{5,7},{6,4},{7,5},{8,10},{9,11},{10,... | collective-permute-start | bytes 786440 | tf_op jit(solution)/shard_map/ppermute | solution.py:20
  21.4 37.7 %collective-permute-start.8 = (f32[2,128,256]{2,1,0:T(8,128)S(1)}, f32[2,128,256]{2,1,0:T(8,128)S(1)}, u32[]{:S(2)}, u32[]{:S(2)}) collective-permute-start(f32[2,128,256]{2,1,0:T(8,128)S(1)} %get-tuple-element.22), channel_id=1, source_target_pairs={{0,3},{1,0},{2,1},{3,2},{4,7},{5,4},{6,5},{7,6},{8,11},{9,8},{10,9... | collective-permute-start | bytes 786440 | tf_op jit(solution)/shard_map/ppermute | solution.py:20
  35.7 31.7 %collective-permute-start.3 = (f32[2,128,256]{2,1,0:T(8,128)S(1)}, f32[2,128,256]{2,1,0:T(8,128)S(1)}, u32[]{:S(2)}, u32[]{:S(2)}) collective-permute-start(f32[2,128,256]{2,1,0:T(8,128)S(1)} %get-tuple-element.10), channel_id=1, source_target_pairs={{0,1},{1,2},{2,3},{3,0},{4,5},{5,6},{6,7},{7,4},{8,9},{9,10},{10,1... | collective-permute-start | bytes 786440 | tf_op jit(solution)/shard_map/ppermute | solution.py:20
  43.9 26.5 %collective-permute-start.4 = (f32[2,128,256]{2,1,0:T(8,128)S(1)}, f32[2,128,256]{2,1,0:T(8,128)S(1)}, u32[]{:S(2)}, u32[]{:S(2)}) collective-permute-start(f32[2,128,256]{2,1,0:T(8,128)S(1)} %get-tuple-element.11), channel_id=1, source_target_pairs={{0,2},{1,3},{2,0},{3,1},{4,6},{5,7},{6,4},{7,5},{8,10},{9,11},{10,... | collective-permute-start | bytes 786440 | tf_op jit(solution)/shard_map/ppermute | solution.py:20
  51.9 18.5 %collective-permute-start.5 = (f32[2,128,256]{2,1,0:T(8,128)S(1)}, f32[2,128,256]{2,1,0:T(8,128)S(1)}, u32[]{:S(2)}, u32[]{:S(2)}) collective-permute-start(f32[2,128,256]{2,1,0:T(8,128)S(1)} %get-tuple-element.12), channel_id=1, source_target_pairs={{0,3},{1,0},{2,1},{3,2},{4,7},{5,4},{6,5},{7,6},{8,11},{9,8},{10,9... | collective-permute-start | bytes 786440 | tf_op jit(solution)/shard_map/ppermute | solution.py:20
  87.2 11.2 %collective-permute-start.12 = (f32[192,512]{1,0:T(8,128)S(1)}, f32[192,512]{1,0:T(8,128)S(1)}, u32[]{:S(2)}, u32[]{:S(2)}) collective-permute-start(f32[192,512]{1,0:T(8,128)S(1)} %constant_dynamic-slice_fusion.7), channel_id=1, source_target_pairs={{0,16},{4,20},{8,24},{12,28},{16,0},{20,4},{24,8},{28,12},{1,17},{... | collective-permute-start | bytes 1179656 | tf_op jit(solution)/shard_map/ppermute | solution.py:25
  87.7 12.3 %collective-permute-start.10 = (f32[192,512]{1,0:T(8,128)S(1)}, f32[192,512]{1,0:T(8,128)S(1)}, u32[]{:S(2)}, u32[]{:S(2)}) collective-permute-start(f32[192,512]{1,0:T(8,128)S(1)} %constant_dynamic-slice_fusion.9), channel_id=1, source_target_pairs={{0,8},{4,12},{8,0},{12,4},{16,24},{20,28},{24,16},{28,20},{1,9},{5... | collective-permute-start | bytes 1179656 | tf_op jit(solution)/shard_map/ppermute | solution.py:25
  98.5 6.2 %collective-permute-start.13 = (f32[96,512]{1,0:T(8,128)S(1)}, f32[96,512]{1,0:T(8,128)S(1)}, u32[]{:S(2)}, u32[]{:S(2)}) collective-permute-start(f32[96,512]{1,0:T(8,128)S(1)} %constant_dynamic-slice_fusion.6), channel_id=1, source_target_pairs={{0,8},{4,12},{8,0},{12,4},{16,24},{20,28},{24,16},{28,20},{1,9},{5... | collective-permute-start | bytes 589832 | tf_op jit(solution)/shard_map/ppermute | solution.py:25
  106.1 9.7 %collective-permute-start.14 = (f32[96,512]{1,0:T(8,128)S(1)}, f32[96,512]{1,0:T(8,128)S(1)}, u32[]{:S(2)}, u32[]{:S(2)}) collective-permute-start(f32[96,512]{1,0:T(8,128)S(1)} %broadcast_select_fusion.2), channel_id=1, source_target_pairs={{0,1},{1,0},{2,3},{3,2},{4,5},{5,4},{6,7},{7,6},{8,9},{9,8},{10,11... | collective-permute-start | bytes 589832 | tf_op jit(solution)/shard_map/ppermute | solution.py:25
  127.4 7.7 %collective-permute-start.17 = (f32[96,512]{1,0:T(8,128)S(1)}, f32[96,512]{1,0:T(8,128)S(1)}, u32[]{:S(2)}, u32[]{:S(2)}) collective-permute-start(f32[96,512]{1,0:T(8,128)S(1)} %maximum_select_fusion.5), channel_id=1, source_target_pairs={{0,1},{1,0},{2,3},{3,2},{4,5},{5,4},{6,7},{7,6},{8,9},{9,8},{10,11... | collective-permute-start | bytes 589832 | tf_op jit(solution)/shard_map/ppermute | solution.py:25
  135.2 7.8 %collective-permute-start.18 = (f32[96,512]{1,0:T(8,128)S(1)}, f32[96,512]{1,0:T(8,128)S(1)}, u32[]{:S(2)}, u32[]{:S(2)}) collective-permute-start(f32[96,512]{1,0:T(8,128)S(1)} %get-tuple-element.45), channel_id=1, source_target_pairs={{0,16},{4,20},{8,24},{12,28},{16,0},{20,4},{24,8},{28,12},{1,17},{... | collective-permute-start | bytes 589832 | tf_op jit(solution)/shard_map/ppermute | solution.py:25
  135.7 7.9 %collective-permute-start.20 = (f32[96,512]{1,0:T(8,128)S(1)}, f32[96,512]{1,0:T(8,128)S(1)}, u32[]{:S(2)}, u32[]{:S(2)}) collective-permute-start(f32[96,512]{1,0:T(8,128)S(1)} %get-tuple-element.46), channel_id=1, source_target_pairs={{0,8},{4,12},{8,0},{12,4},{16,24},{20,28},{24,16},{28,20},{1,9},{5... | collective-permute-start | bytes 589832 | tf_op jit(solution)/shard_map/ppermute | solution.py:25
  143.0 7.8 %collective-permute-start.19 = (f32[192,512]{1,0:T(8,128)S(1)}, f32[192,512]{1,0:T(8,128)S(1)}, u32[]{:S(2)}, u32[]{:S(2)}) collective-permute-start(f32[192,512]{1,0:T(8,128)S(1)} %maximum_select_fusion.3), channel_id=1, source_target_pairs={{0,8},{4,12},{8,0},{12,4},{16,24},{20,28},{24,16},{28,20},{1,9},{5... | collective-permute-start | bytes 1179656 | tf_op jit(solution)/shard_map/ppermute | solution.py:25
  143.7 7.8 %collective-permute-start.21 = (f32[192,512]{1,0:T(8,128)S(1)}, f32[192,512]{1,0:T(8,128)S(1)}, u32[]{:S(2)}, u32[]{:S(2)}) collective-permute-start(f32[192,512]{1,0:T(8,128)S(1)} %maximum_select_fusion.4), channel_id=1, source_target_pairs={{0,16},{4,20},{8,24},{12,28},{16,0},{20,4},{24,8},{28,12},{1,17},{... | collective-permute-start | bytes 1179656 | tf_op jit(solution)/shard_map/ppermute | solution.py:25
  151.9 9.1 %collective-permute-start.23 = (f32[128,128]{1,0:T(8,128)S(1)}, f32[128,128]{1,0:T(8,128)S(1)}, u32[]{:S(2)}, u32[]{:S(2)}) collective-permute-start(f32[128,128]{1,0:T(8,128)S(1)} %bitcast.42), channel_id=1, source_target_pairs={{0,1},{1,2},{2,3},{3,0},{4,5},{5,6},{6,7},{7,4},{8,9},{9,10},{10,1... | collective-permute-start | bytes 196616 | tf_op jit(solution)/shard_map/ppermute | solution.py:20
  153.9 7.2 %collective-permute-start.24 = (f32[128,128]{1,0:T(8,128)S(1)}, f32[128,128]{1,0:T(8,128)S(1)}, u32[]{:S(2)}, u32[]{:S(2)}) collective-permute-start(f32[128,128]{1,0:T(8,128)S(1)} %bitcast.43), channel_id=1, source_target_pairs={{0,2},{1,3},{2,0},{3,1},{4,6},{5,7},{6,4},{7,5},{8,10},{9,11},{10,... | collective-permute-start | bytes 196616 | tf_op jit(solution)/shard_map/ppermute | solution.py:20
  175.5 10.2 %collective-permute-start.26 = (f32[2,64,768]{2,1,0:T(8,128)}, f32[2,64,768]{2,1,0:T(8,128)S(1)}, u32[]{:S(2)}, u32[]{:S(2)}) collective-permute-start(f32[2,64,768]{2,1,0:T(8,128)} %beams.1), channel_id=1, source_target_pairs={{0,4},{4,8},{8,12},{12,16},{16,20},{20,24},{24,28},{1,5},{5,9},{9,... | collective-permute-start | bytes 1179656 | tf_op jit(solution)/shard_map/ppermute | solution.py:31
  186.9 7.1 %collective-permute-start.27 = (f32[2,48,256]{2,1,0:T(8,128)S(1)}, f32[2,48,256]{2,1,0:T(8,128)S(1)}, u32[]{:S(2)}, u32[]{:S(2)}) collective-permute-start(f32[2,48,256]{2,1,0:T(8,128)S(1)} %bitcast.39), channel_id=1, source_target_pairs={{0,1},{1,2},{2,3},{3,0},{4,5},{5,6},{6,7},{7,4},{8,9},{9,10},{10,1... | collective-permute-start | bytes 294920 | tf_op jit(solution)/shard_map/ppermute | solution.py:20
  188.3 8.5 %collective-permute-start.28 = (f32[2,48,256]{2,1,0:T(8,128)S(1)}, f32[2,48,256]{2,1,0:T(8,128)S(1)}, u32[]{:S(2)}, u32[]{:S(2)}) collective-permute-start(f32[2,48,256]{2,1,0:T(8,128)S(1)} %bitcast.40), channel_id=1, source_target_pairs={{0,2},{1,3},{2,0},{3,1},{4,6},{5,7},{6,4},{7,5},{8,10},{9,11},{10,... | collective-permute-start | bytes 294920 | tf_op jit(solution)/shard_map/ppermute | solution.py:20
  190.2 6.5 %collective-permute-start.29 = (f32[2,48,256]{2,1,0:T(8,128)S(1)}, f32[2,48,256]{2,1,0:T(8,128)S(1)}, u32[]{:S(2)}, u32[]{:S(2)}) collective-permute-start(f32[2,48,256]{2,1,0:T(8,128)S(1)} %bitcast.41), channel_id=1, source_target_pairs={{0,3},{1,0},{2,1},{3,2},{4,7},{5,4},{6,5},{7,6},{8,11},{9,8},{10,9... | collective-permute-start | bytes 294920 | tf_op jit(solution)/shard_map/ppermute | solution.py:20
  (24 other events, 118.5 us)

commit v2 on v1

v2 whole, which is shorter than its diff:
```python
import math

import jax
import jax.numpy as jnp
from jax import lax
from jax.experimental import pallas as pl
from jax.experimental.pallas import tpu as pltpu
from jax.sharding import PartitionSpec as P


ITERS = 3
EPS = 1e-06
F32 = jnp.float32
BF16 = jnp.bfloat16
NT = (((1,), (1,)), ((), ()))
NN = (((1,), (0,)), ((), ()))


def crossed(x, axis, mask):
    return lax.ppermute(x, axis, [(i, i ^ mask) for i in range(lax.axis_size(axis))])


def swapped(x, axis, bit):
    return crossed(x, axis, 1 << bit)


def bits(axis):
    return list(range(lax.axis_size(axis).bit_length() - 1))


def from_behind(x, axis, by):
    devices = lax.axis_size(axis)
    pairs = [(i, i + by) for i in range(devices) if 0 <= i + by < devices]
    return lax.ppermute(x, axis, pairs)


def bit_of(index, bit):
    return (index >> bit) & 1


def joined(own, other, flag):
    return jnp.where(
        flag == 0, jnp.concatenate([own, other], 0), jnp.concatenate([other, own], 0)
    )


def gather_step(x, axis, bit):
    return joined(x, swapped(x, axis, bit), bit_of(lax.axis_index(axis), bit))


def summed_everywhere(keep, send):
    rest = bits("tm")[1:]
    orders = (rest, rest[::-1])
    index = lax.axis_index("tm")
    sums, cut = (keep, swapped(send, "tm", 0)), 2
    for step in range(len(rest)):
        flags = jnp.stack([bit_of(index, order[step]) for order in orders])
        kept, sent = add_split(cut, flags, *sums)
        got = [swapped(part, "tm", order[step]) for part, order in zip(sent, orders)]
        sums, cut = (kept[0], got[0], kept[1], got[1]), 1
    flag = bit_of(lax.axis_index("elem"), 0)
    x, sent = add_choose(flag, *sums)
    x = x + swapped(sent, "elem", 0)
    for bit in bits("elem")[1:]:
        x = x + swapped(x, "elem", bit)
    other = swapped(x, "elem", 0)
    parts = [jnp.where(flag == 0, x, other), jnp.where(flag == 0, other, x)]
    for step in range(len(rest) - 1, -1, -1):
        parts = [gather_step(part, "tm", order[step]) for part, order in zip(parts, orders)]
    return parts, [swapped(part, "tm", 0) for part in parts]


def split(x):
    high = x.astype(BF16)
    return high, (x - high.astype(F32)).astype(BF16)


def split_kept(x):
    high = lax.reduce_precision(x, 8, 7)
    return high.astype(BF16), (x - high).astype(BF16)


def dot(left, right, dims):
    return lax.dot_general(left, right, dims, preferred_element_type=F32)


def triple(left, right, dims):
    return (
        dot(left[0], right[0], dims) + dot(left[0], right[1], dims) + dot(left[1], right[0], dims)
    )


REAL, IMAG, MINUS, MOD_REAL, MOD_IMAG = range(5)


def prepare(place_ref, pieces, cs_ref, lefts):
    n = lefts[0].shape[0] // len(pieces)
    cosine, sine = cs_ref[0:1, :], cs_ref[1:2, :]
    for k, piece in enumerate(pieces):
        rows = pl.ds(pl.multiple_of(place_ref[k] * n, n), n)
        real, imag = piece[0, 0:n, :], piece[1, 0:n, :]
        for where, value in (
            (REAL, real),
            (IMAG, imag),
            (MINUS, -imag),
            (MOD_REAL, real * cosine + imag * sine),
            (MOD_IMAG, imag * cosine - real * sine),
        ):
            lefts[2 * where][rows, :], lefts[2 * where + 1][rows, :] = split(value)


def half_product(h, lefts, acc_ref, out_ref):
    elems = lefts[0].shape[0]
    half = elems // 2
    mine = pl.ds(pl.multiple_of(h * half, half), half)
    others = pl.ds(pl.multiple_of((1 - h) * half, half), half)
    everything = pl.ds(0, elems)

    def rows(where, at):
        return tuple(lefts[2 * where + part][at, :] for part in range(2))

    def put(top, cols, value):
        at = (pl.ds(top, half), cols)
        if acc_ref is not None:
            value = value + acc_ref[at]
        out_ref[at] = value

    def real_part(left, at):
        return triple(left[0], rows(REAL, at), NT) + triple(left[1], rows(IMAG, at), NT)

    def imag_part(left, at):
        return triple(left[1], rows(REAL, at), NT) + triple(left[0], rows(MINUS, at), NT)

    mod = (rows(MOD_REAL, mine), rows(MOD_IMAG, mine))
    put(0, everything, real_part(mod, everything))
    put(half, everything, imag_part(mod, everything))
    above = lax.broadcasted_iota(jnp.int32, (half, half), 0) <= lax.broadcasted_iota(
        jnp.int32, (half, half), 1
    )
    plain = (rows(REAL, mine), rows(IMAG, mine))
    put(2 * half, mine, jnp.where(above, real_part(plain, mine), imag_part(plain, mine)))

    @pl.when(h == 0)
    def _():
        put(2 * half, others, real_part(plain, others))

    @pl.when(h != 0)
    def _():
        put(2 * half, others, imag_part(plain, others))


def gram_kernel(has_acc, place_ref, core_ref, *refs):
    pieces, cs_ref, refs = refs[:4], refs[4], refs[5:]
    accs, refs = (refs[:2], refs[2:]) if has_acc else ((None, None), refs)
    prepare(place_ref, pieces, cs_ref, refs[2:])
    half_product(1 - core_ref[0], refs[2:], accs[0], refs[0])
    half_product(core_ref[0], refs[2:], accs[1], refs[1])


SMEM_SPEC = pl.BlockSpec(memory_space=pltpu.SMEM)
VMEM_SPEC = pl.BlockSpec(memory_space=pltpu.VMEM)
MIB = 1 << 20


def gram(elems, place, core, pieces, cs, accs):
    count = pieces[0].shape[2]
    args = [*pieces, cs, *(accs or ())]
    return pl.pallas_call(
        lambda *refs: gram_kernel(accs is not None, *refs),
        out_shape=[jax.ShapeDtypeStruct((3 * elems // 2, elems), F32)] * 2,
        in_specs=[SMEM_SPEC] * 2 + [VMEM_SPEC] * len(args),
        out_specs=[VMEM_SPEC] * 2,
        scratch_shapes=[pltpu.VMEM((elems, count), BF16)] * 10,
        input_output_aliases={7: 0, 8: 1} if accs else {},
        compiler_params=pltpu.CompilerParams(vmem_limit_bytes=24 * MIB),
        cost_estimate=pl.CostEstimate(
            flops=42 * elems * elems * count, bytes_accessed=16 * elems * elems, transcendentals=0
        ),
        name="gram",
    )(place, core, *args)


def add_split_kernel(cut, flags_ref, *refs):
    count = len(refs) // (2 + 2 * cut)
    outs = refs[2 * count :]
    for i in range(count):
        x, y = refs[2 * i], refs[2 * i + 1]
        half = x.shape[0] // (2 * cut)
        for part in range(cut):
            at = i * cut + part
            for side in range(2):
                chosen = flags_ref[at] if side == 0 else 1 - flags_ref[at]
                rows = pl.ds(pl.multiple_of((2 * part + chosen) * half, half), half)
                outs[2 * at + side][...] = x[rows, :] + y[rows, :]


def add_choose_kernel(flag_ref, a, b, c, d, kept_ref, sent_ref):
    @pl.when(flag_ref[0] == 0)
    def _():
        kept_ref[...] = a[...] + b[...]
        sent_ref[...] = c[...] + d[...]

    @pl.when(flag_ref[0] != 0)
    def _():
        kept_ref[...] = c[...] + d[...]
        sent_ref[...] = a[...] + b[...]


def add_choose(flag, *pairs):
    return pl.pallas_call(
        add_choose_kernel,
        out_shape=[jax.ShapeDtypeStruct(pairs[0].shape, F32)] * 2,
        in_specs=[SMEM_SPEC] + [VMEM_SPEC] * 4,
        out_specs=[VMEM_SPEC] * 2,
        compiler_params=pltpu.CompilerParams(vmem_limit_bytes=8 * MIB),
        name="add_choose",
    )(flag[None], *pairs)


def add_split(cut, flags, *pairs):
    shape = (pairs[0].shape[0] // (2 * cut), pairs[0].shape[1])
    if shape[0] % 8:
        sums = [x + y for x, y in zip(pairs[0::2], pairs[1::2])]
        parts = [part for x in sums for part in jnp.split(x, cut)]
        return tuple(
            [
                lax.dynamic_slice_in_dim(part, jnp.abs(side - flags[at]) * shape[0], shape[0], 0)
                for at, part in enumerate(parts)
            ]
            for side in range(2)
        )
    out = pl.pallas_call(
        lambda *refs: add_split_kernel(cut, *refs),
        out_shape=[jax.ShapeDtypeStruct(shape, F32)] * (len(pairs) * cut),
        in_specs=[SMEM_SPEC] + [VMEM_SPEC] * len(pairs),
        out_specs=[VMEM_SPEC] * (len(pairs) * cut),
        compiler_params=pltpu.CompilerParams(vmem_limit_bytes=12 * MIB),
        name="add_split",
    )(flags, *pairs)
    return out[0::2], out[1::2]


def power_kernel(total, core_ref, *refs):
    parts, v_ref, out_ref = refs[:4], refs[4], refs[5]
    cr, ci, pr, pi, packed_ref = refs[6:8], refs[8:10], refs[10:12], refs[12:14], refs[14]
    elems = v_ref.shape[1] // 2
    half = elems // 2
    beams = v_ref.shape[0]
    rows = 2 * beams
    scale = 1.0 / math.sqrt(total * elems)

    for other in range(2):
        h = core_ref[0] if other == 0 else 1 - core_ref[0]
        for part in range(2):
            ref = parts[2 * other + part]
            length = ref.shape[0]
            for begin in range(0, length, half // 2):
                row = part * length + begin
                at = pl.ds(pl.multiple_of(h * half, half) + row % half, half // 2)
                value = ref[pl.ds(begin, half // 2), :]
                if row < 2 * half:
                    pair = cr if row < half else ci
                    pair[0][at, :], pair[1][at, :] = split(value * scale)
                else:
                    packed_ref[at, :] = value * (1.0 / total)

    def store(pair, value):
        pair[0][...], pair[1][...] = split(value)

    packed = packed_ref[...]
    mirrored = packed.T
    row = lax.broadcasted_iota(jnp.int32, (elems, elems), 0)
    col = lax.broadcasted_iota(jnp.int32, (elems, elems), 1)
    store(pr, jnp.where(row <= col, packed, mirrored))
    store(pi, jnp.where(row > col, packed, jnp.where(row < col, -mirrored, 0.0)))

    def normalized(v):
        squares = jnp.sum(v * v, axis=1, keepdims=True)
        squares = squares[:beams] + squares[beams:]
        inverse = 1.0 / jnp.sqrt(squares + EPS)
        return v * jnp.concatenate([inverse, inverse], 0)

    def times(v, pair, dims):
        high, low = split(v)
        both = dot(jnp.concatenate([high, low], 0), pair[0][...], dims)
        return both[:rows] + both[rows:] + dot(high, pair[1][...], dims)

    v = normalized(jnp.concatenate([v_ref[:, 0:elems], v_ref[:, elems:]], 0) - 4.5)
    for _ in range(ITERS):
        by_real = times(v, cr, NN)
        by_imag = times(v, ci, NN)
        w = jnp.concatenate(
            [by_real[:beams] + by_imag[beams:], by_real[beams:] - by_imag[:beams]], 0
        )
        by_real = times(w, cr, NT) + times(v, pr, NT)
        by_imag = times(w, ci, NT) + times(v, pi, NT)
        v = normalized(
            jnp.concatenate(
                [by_real[:beams] - by_imag[beams:], by_real[beams:] + by_imag[:beams]], 0
            )
        )
    out_ref[...] = v


def power(total, core, parts, start):
    rows, elems = 2 * start.shape[0], start.shape[1] // 2
    return pl.pallas_call(
        lambda *refs: power_kernel(total, *refs),
        out_shape=jax.ShapeDtypeStruct((rows, elems), F32),
        in_specs=[SMEM_SPEC] + [VMEM_SPEC] * 5,
        out_specs=VMEM_SPEC,
        scratch_shapes=[pltpu.VMEM((elems, elems), BF16)] * 8 + [pltpu.VMEM((elems, elems), F32)],
        compiler_params=pltpu.CompilerParams(vmem_limit_bytes=24 * MIB),
        cost_estimate=pl.CostEstimate(
            flops=ITERS * 36 * elems * elems * rows, bytes_accessed=16 * elems * elems, transcendentals=0
        ),
        name="power",
    )(core, *parts, start)


def beam_kernel(place_ref, v_ref, *refs):
    pieces, out_ref = refs[:-1], refs[-1]
    rows = v_ref.shape[0]
    beams = rows // 2
    n = v_ref.shape[1] // 4
    count = pieces[0].shape[2]
    lefts = []
    for k in range(4):
        v = v_ref[:, pl.ds(pl.multiple_of(place_ref[k] * n, n), n)]
        high, low = split(v)
        lefts.append((jnp.concatenate([high, low], 0), high))
    for chunk in range(len(pieces) // 4):
        totals = []
        for half in range(2):
            total = 0.0
            for k in range(4):
                high, low = split(pieces[4 * chunk + k][half, 0:n, :])
                both = dot(lefts[k][0], high, NN)
                total = total + (both[:rows] + both[rows:] + dot(lefts[k][1], low, NN))
            totals.append(total)
        by_real, by_imag = totals
        cols = pl.ds(chunk * count, count)
        out_ref[0, :, cols] = by_real[:beams] + by_imag[beams:]
        out_ref[1, :, cols] = by_imag[:beams] - by_real[beams:]


def beams_of(place, v, pieces):
    beams = v.shape[0] // 2
    count = pieces[0].shape[2] * (len(pieces) // 4)
    return pl.pallas_call(
        beam_kernel,
        out_shape=jax.ShapeDtypeStruct((2, beams, count), F32),
        in_specs=[SMEM_SPEC] + [VMEM_SPEC] * (1 + len(pieces)),
        out_specs=VMEM_SPEC,
        compiler_params=pltpu.CompilerParams(vmem_limit_bytes=24 * MIB),
        name="beams",
    )(place, v, *pieces)


def dft_kernel(place_ref, *refs):
    pieces = refs[:4]
    ch, cl, sh, sl, out_ref = refs[4:]
    rows, count = pieces[0].shape[1:]
    width = ch.shape[1]
    phase = lax.broadcasted_iota(jnp.int32, (2 * rows, count), 1) % 4
    by_cos, by_sin = 0.0, 0.0
    for k, piece in enumerate(pieces):
        where = pl.ds(pl.multiple_of(place_ref[k] * count, count), count)
        w = jnp.concatenate([piece[0], piece[1]], 0)
        high, low = split(jnp.concatenate([jnp.where(phase == j, w, 0.0) for j in range(4)], 0))
        by_cos = by_cos + triple((high, low), (ch[where, :], cl[where, :]), NN)
        by_sin = by_sin + triple((high, low), (sh[where, :], sl[where, :]), NN)
    real, imag = [], []
    for j in range(4):
        top, mid, end = 2 * rows * j, 2 * rows * j + rows, 2 * rows * (j + 1)
        real.append(by_cos[top:mid] + by_sin[mid:end])
        imag.append(by_cos[mid:end] - by_sin[top:mid])
    for q in range(4):
        total_real, total_imag = 0.0, 0.0
        for j in range(4):
            turned = (
                (real[j], imag[j]),
                (imag[j], -real[j]),
                (-real[j], -imag[j]),
                (-imag[j], real[j]),
            )[q * j % 4]
            total_real, total_imag = total_real + turned[0], total_imag + turned[1]
        out_ref[0, :, pl.ds(q * width, width)] = total_real
        out_ref[1, :, pl.ds(q * width, width)] = total_imag


def dft(place, pieces, tables):
    rows = pieces[0].shape[1]
    channels = tables[0].shape[0]
    return pl.pallas_call(
        dft_kernel,
        out_shape=jax.ShapeDtypeStruct((2, rows, channels), F32),
        in_specs=[SMEM_SPEC] + [VMEM_SPEC] * 8,
        out_specs=VMEM_SPEC,
        compiler_params=pltpu.CompilerParams(vmem_limit_bytes=16 * MIB),
        name="dft",
    )(place, *pieces, *tables)


def rotation(shift_bin, times, modulus):
    folded = shift_bin[0] * times % modulus
    angle = 2.0 * math.pi / modulus * folded.astype(F32)
    return jnp.stack([jnp.cos(angle), jnp.sin(angle)])


def dft_tables(channels, width):
    step = 32
    f = lax.iota(jnp.int32, width)[None, :]

    def rows(count, factor):
        k = factor * lax.iota(jnp.int32, count)[:, None] * f % channels
        angle = 2.0 * math.pi / channels * k.astype(F32)
        return jnp.cos(angle), jnp.sin(angle)

    coarse, fine = rows(channels // step, step), rows(step, 1)
    a_cos, a_sin = (t[:, None, :] for t in coarse)
    b_cos, b_sin = (t[None, :, :] for t in fine)
    norm = 1.0 / math.sqrt(channels)
    cosine = ((a_cos * b_cos - a_sin * b_sin) * norm).reshape(channels, width)
    sine = ((a_sin * b_cos + a_cos * b_sin) * norm).reshape(channels, width)
    return (*split_kept(cosine), *split_kept(sine))


def share_of_start(start_vectors, width):
    shares, index = lax.axis_size("tm"), lax.axis_index("tm")
    rows = start_vectors.astype(F32).transpose(0, 2, 1)
    count = rows.shape[1] // shares
    rows = lax.dynamic_slice_in_dim(rows, index * count, count, 1)
    return jnp.pad(rows, ((0, 0), (0, -count % 8), (0, width - rows.shape[2])))


def gathered_start(pieces, place, n, beams):
    count = beams // lax.axis_size("tm")
    joint = jnp.zeros((2, count, n * len(pieces)), F32)
    for k, piece in enumerate(pieces):
        share = piece[:, n : n + count, 0:n]
        joint = lax.dynamic_update_slice(joint, share, (0, 0, place[k] * n))
    joint = jnp.concatenate([joint[0], joint[1]], 1)
    for bit in bits("tm"):
        joint = gather_step(joint, "tm", bit)
    return joint


def body(samples, shift_bin, start_vectors, tap_table):
    taps_count, channels = tap_table.shape
    elems_dev, span_len = samples.shape[1:]
    devices = lax.axis_size("elem")
    modulus = span_len * lax.axis_size("tm")
    frames = span_len // channels
    quarter = channels // devices
    mine = lax.axis_index("elem")
    span_start = lax.axis_index("tm") * span_len
    place = jnp.stack([mine ^ k for k in range(devices)])
    core = (lax.axis_index("tm") & 1)[None]

    chunks = []
    accs = None
    late = samples
    for frame in range(frames):
        own = []
        for k in range(devices):
            begin = frame * channels + (mine ^ k) * quarter
            own.append(lax.dynamic_slice_in_dim(late, begin, quarter, 2))
        if frame == 0:
            share = share_of_start(start_vectors, quarter)
            own = [jnp.concatenate([part, share], 1) for part in own]
            late, own = lax.optimization_barrier((late, own))
        pieces = own[:1]
        for k in range(1, devices):
            pieces.append(crossed(own[k], "elem", k))
        times = span_start + frame * channels + mine * quarter + lax.iota(jnp.int32, quarter)
        rotated = rotation(shift_bin, times, modulus)
        if frame == min(1, frames - 1):
            tables, start = dft_tables(channels, quarter), gathered_start(
                chunks[0], place, elems_dev, start_vectors.shape[2]
            )
            rotated, tables, start = lax.optimization_barrier((rotated, tables, start))
        accs = gram(elems_dev * devices, place, core, pieces, rotated, accs)
        chunks.append(pieces)
    sent, kept = accs

    own_parts, other_parts = summed_everywhere(kept, sent)
    v = power(modulus, core, (*own_parts, *other_parts), start)
    beams = v.shape[0] // 2
    weights = (
        lax.dynamic_slice_in_dim(v, mine * elems_dev, elems_dev, 1)
        .reshape(2, beams, elems_dev)
        .transpose(0, 2, 1)
    )
    b = beams_of(place, v, [piece for pieces in chunks for piece in pieces])
    extended = jnp.concatenate([from_behind(b[:, :, -(taps_count - 1) * quarter :], "tm", 1), b], 2)
    taps = lax.dynamic_slice_in_dim(tap_table, mine * quarter, quarter, 1).astype(F32) / 2048.0
    folded = []
    for frame in range(frames):
        w = 0.0
        for tap in range(taps_count):
            at = taps_count - 1 + frame - tap
            w = w + taps[tap] * extended[:, :, at * quarter : (at + 1) * quarter]
        folded.append(w)
    folded = jnp.stack(folded, 1)
    beams_dev = beams // devices
    received = []
    for k in range(devices):
        part = lax.dynamic_slice_in_dim(folded, (mine ^ k) * beams_dev, beams_dev, 2)
        part = part.reshape(2, frames * beams_dev, quarter)
        received.append(part if k == 0 else crossed(part, "elem", k))
    spectra = dft(place, received, tables)
    spectra = spectra.reshape(2, frames, beams_dev, channels).transpose(0, 2, 1, 3)
    return (spectra, weights.reshape(2, elems_dev, beams))


def solution(mesh):
    return jax.shard_map(
        body,
        mesh=mesh,
        in_specs=(P(None, "elem", "tm"), P(), P(None, "elem", None), P()),
        out_specs=(P(None, "elem", "tm", None), P(None, "elem", None)),
        check_vma=False,
    )
```

time: 204 us -> 185 us (0.907)
  other arithmetic: 18.7 us -> 6.32 us
  Pallas kernels: 40.4 us -> 30.3 us
  starting transfers between devices: 52.1 us -> 59.2 us
  local copies, waits for them, and re-layouts: 11.6 us -> 7.73 us
    ppermute x29, starting transfers between devices: 50.2 us -> 57.1 us  [crossed(): lax.ppermute(x, axis, [(i, i ^ mask) for i in range(lax.axis_size(axis))])]
    pallas_call x4 -> x7, Pallas kernels: 27.2 us -> 20.8 us  [the longest x3 16 us: gram(): pl.pallas_call(lambda *refs: gram_kernel(accs is not None, *refs), out_sh...]
    convert_element_type x1, other arithmetic: 5.06 us -> 0.36 us  [split_kept(): return (high.astype(BF16), (x - high).astype(BF16))]
    select_n x6 -> x7, other arithmetic: 4.37 us -> 0.96 us  [joined(): jnp.where(flag == 0, jnp.concatenate([own, other], 0), jnp.concatenate([o...]
    dynamic_slice x12 -> x7, local copies, waits for them, and re-layouts: 6.79 us -> 4 us  [the longest x2 3.93 us: body(): own.append(lax.dynamic_slice_in_dim(late, begin, quarter, 2))]
    pallas_call x1, Pallas kernels: 9.12 us -> 6.81 us  [power(): pl.pallas_call(lambda *refs: power_kernel(total, *refs), out_shape=jax.Sh...]
  transfers between devices with their start and end apart: 30 -> 30, of which waited for: 19 -> 21; matrix products, arithmetic and copies ran while one was open for 9% -> 5% of each run, Pallas kernels for 7% -> 6%
where the time goes in v2:
time: 185 us; the launch traced here: 184 us
  waiting for transfers between devices  78.7 us (43%)
  starting transfers between devices  59.2 us (32%)
  Pallas kernels  30.3 us (16%)
  local copies, waits for them, and re-layouts  7.73 us (4%)
  other arithmetic  6.32 us (3%)
    ppermute x29, waiting for transfers between devices, crossed(): lax.ppermute(x, axis, [(i, i ^ mask) for i in range(lax.axis_size(axis))])  71.5 us
    ppermute x29, starting transfers between devices, crossed(): lax.ppermute(x, axis, [(i, i ^ mask) for i in range(lax.axis_size(axis))])  57.1 us
    pallas_call x3, Pallas kernels, gram(): pl.pallas_call(lambda *refs: gram_kernel(accs is not None, *refs), out_sh...  16 us
    ppermute x1, waiting for transfers between devices, from_behind(): return lax.ppermute(x, axis, pairs)  7.23 us
    pallas_call x1, Pallas kernels, power(): pl.pallas_call(lambda *refs: power_kernel(total, *refs), out_shape=jax.Sh...  6.81 us
    dynamic_slice x2, local copies, waits for them, and re-layouts, body(): own.append(lax.dynamic_slice_in_dim(late, begin, quarter, 2))  3.93 us
  transfers between devices with their start and end apart: 30, of which 21 were waited for; matrix products, arithmetic and copies ran while one was open for 5% of the time, Pallas kernels for 6%

profile of v2, /device:TPU:4, one launch (start us, length us, event | category | flops | bytes accessed | tf_op | source)
XLA Modules:
  0.0 184.0 jit_solution(2370123559381350934)
XLA Ops:
  7.9 2.7 %constant_dynamic-slice_fusion.5 = (f32[2,128,256]{2,1,0:T(8,128)}, f32[2,128,256]{2,1,0:T(8,128)}, f32[2,128,256]{2,1,0:T(8,128)}, f32[2,128,256]{2,1,0:T(8,128...) fusion(f32[2,128,3072]{2,1,0:T(8,128)} %param.4, ...), kind=kLoop, calls=%fused_computation.69 | loop fusion | bytes 4194336 | tf_op jit(solution)/shard_map/dynamic_slice | solution.py:468
  11.3 3.5 %collective-permute-start.4 = (f32[2,128,256]{2,1,0:T(8,128)}, f32[2,128,256]{2,1,0:T(8,128)}, u32[]{:S(2)}, u32[]{:S(2)}) collective-permute-start(f32[2,128,256]{2,1,0:T(8,128)} %get-tuple-element.57), channel_id=1, source_target_pairs={{0,2},{1,3},{2,0},{3,1},{4,6},{5,7},{6,4},{7,5},{8,10},{9,11},{10,... | collective-permute-start | bytes 786440 | tf_op jit(solution)/shard_map/ppermute | solution.py:20
  18.5 4.1 %collective-permute-start.5 = (f32[2,128,256]{2,1,0:T(8,128)}, f32[2,128,256]{2,1,0:T(8,128)}, u32[]{:S(2)}, u32[]{:S(2)}) collective-permute-start(f32[2,128,256]{2,1,0:T(8,128)} %get-tuple-element.56), channel_id=1, source_target_pairs={{0,3},{1,2},{2,1},{3,0},{4,7},{5,6},{6,5},{7,4},{8,11},{9,10},{10,... | collective-permute-start | bytes 786440 | tf_op jit(solution)/shard_map/ppermute | solution.py:20
  22.6 5.2 %collective-permute-done.7.refs_4_.refs_2_ = f32[2,136,256]{2,1,0:T(8,128)} collective-permute-done((f32[2,136,256]{2,1,0:T(8,128)}, f32[2,136,256]{2,1,0:T(8,128)}, u32[]{:S(2)}, u32[]{:S(2)}) %collective-permute-start.7) | collective-permute-done | bytes 278560 | tf_op jit(solution)/shard_map/ppermute | solution.py:20
  32.2 2.7 %collective-permute-done.10 = f32[16,1024]{1,0:T(8,128)S(1)} collective-permute-done((f32[16,1024]{1,0:T(8,128)S(1)}, f32[16,1024]{1,0:T(8,128)S(1)}, u32[]{:S(2)}, u32[]{:S(2)}) %collective-permute-start.10) | collective-permute-done | bytes 65568 | tf_op jit(solution)/shard_map/ppermute | solution.py:20
  35.5 5.1 %gram.3 = (f32[768,512]{1,0:T(8,128)S(1)}, f32[768,512]{1,0:T(8,128)S(1)}) custom-call(s32[4]{0:T(128)S(1)} %pad_add_fusion.refs_0_.place_ref, s32[1]{0:T(128)} %bitcast.5.refs_1_.refs_0_, f32[2,136,256]{2,1,0:T(8,128)S(1)} %get-tuple-element.30.refs_2_.refs_0_, f32[2,136,256]{2,1,0:T(8,128)S(1)} %collective-permute-done.6.refs_3_.refs_1_, ...), custom_call_target="tpu_custom_call" | custom-call | flops 2818572288 | bytes 4194304 | tf_op jit(solution)/shard_map/gram/pallas_call | solution.py:168
  40.6 18.1 %collective-permute-start.1 = (f32[2,128,256]{2,1,0:T(8,128)S(1)}, f32[2,128,256]{2,1,0:T(8,128)S(1)}, u32[]{:S(2)}, u32[]{:S(2)}) collective-permute-start(f32[2,128,256]{2,1,0:T(8,128)S(1)} %copy-done.15), channel_id=1, source_target_pairs={{0,2},{1,3},{2,0},{3,1},{4,6},{5,7},{6,4},{7,5},{8,10},{9,11},{10,... | collective-permute-start | bytes 786440 | tf_op jit(solution)/shard_map/ppermute | solution.py:20
  60.9 5.3 %gram.4 = (f32[768,512]{1,0:T(8,128)S(1)}, f32[768,512]{1,0:T(8,128)S(1)}) custom-call(s32[4]{0:T(128)S(1)} %pad_add_fusion.refs_0_.place_ref, s32[1]{0:T(128)} %bitcast.5.refs_1_.refs_0_, f32[2,128,256]{2,1,0:T(8,128)S(1)} %get-tuple-element.59.refs_2_.refs_4_, ...), custom_call_target="tpu_custom_call", output_to_operand_aliasing={{0}: (7, {}), {1}: (8, {})} | custom-call | flops 2818572288 | bytes 4194304 | tf_op jit(solution)/shard_map/gram/pallas_call | solution.py:168
  66.2 10.1 %collective-permute-done.1.refs_4_.refs_10_ = f32[2,128,256]{2,1,0:T(8,128)S(1)} collective-permute-done((f32[2,128,256]{2,1,0:T(8,128)S(1)}, f32[2,128,256]{2,1,0:T(8,128)S(1)}, u32[]{:S(2)}, u32[]{:S(2)}) %collective-permute-start.1) | collective-permute-done | bytes 262176 | tf_op jit(solution)/shard_map/ppermute | solution.py:20
  76.3 5.6 %gram.5 = (f32[768,512]{1,0:T(8,128)S(1)}, f32[768,512]{1,0:T(8,128)S(1)}) custom-call(s32[4]{0:T(128)S(1)} %pad_add_fusion.refs_0_.place_ref, s32[1]{0:T(128)} %bitcast.5.refs_1_.refs_0_, f32[2,128,256]{2,1,0:T(8,128)S(1)} %get-tuple-element.63.refs_2_.refs_8_, ...), custom_call_target="tpu_custom_call", output_to_operand_aliasing={{0}: (7, {}), {1}: (8, {})} | custom-call | flops 2818572288 | bytes 4194304 | tf_op jit(solution)/shard_map/gram/pallas_call | solution.py:168
  82.1 3.3 %collective-permute-done.12.refs_2_ = f32[768,512]{1,0:T(8,128)S(1)} collective-permute-done((f32[768,512]{1,0:T(8,128)S(1)}, f32[768,512]{1,0:T(8,128)S(1)}, u32[]{:S(2)}, u32[]{:S(2)}) %collective-permute-start.12) | collective-permute-done | bytes 1572896 | tf_op jit(solution)/shard_map/ppermute | solution.py:20
  89.3 8.1 %collective-permute-done.13.refs_2_ = f32[192,512]{1,0:T(8,128)S(1)} collective-permute-done((f32[192,512]{1,0:T(8,128)S(1)}, f32[192,512]{1,0:T(8,128)S(1)}, u32[]{:S(2)}, u32[]{:S(2)}) %collective-permute-start.13) | collective-permute-done | bytes 393248 | tf_op jit(solution)/shard_map/ppermute | solution.py:20
  102.7 4.0 %collective-permute-done.15.b = f32[96,512]{1,0:T(8,128)S(1)} collective-permute-done((f32[96,512]{1,0:T(8,128)}, f32[96,512]{1,0:T(8,128)S(1)}, u32[]{:S(2)}, u32[]{:S(2)}) %collective-permute-start.15) | collective-permute-done | bytes 196640 | tf_op jit(solution)/shard_map/ppermute | solution.py:20
  109.0 5.0 %collective-permute-start.17 = (f32[96,512]{1,0:T(8,128)S(1)}, f32[96,512]{1,0:T(8,128)S(1)}, u32[]{:S(2)}, u32[]{:S(2)}) collective-permute-start(f32[96,512]{1,0:T(8,128)S(1)} %get-tuple-element.50), channel_id=1, source_target_pairs={{0,1},{1,0},{2,3},{3,2},{4,5},{5,4},{6,7},{7,6},{8,9},{9,8},{10,11... | collective-permute-start | bytes 589832 | tf_op jit(solution)/shard_map/ppermute | solution.py:20
  114.0 3.9 %collective-permute-done.17 = f32[96,512]{1,0:T(8,128)S(1)} collective-permute-done((f32[96,512]{1,0:T(8,128)S(1)}, f32[96,512]{1,0:T(8,128)S(1)}, u32[]{:S(2)}, u32[]{:S(2)}) %collective-permute-start.17) | collective-permute-done | bytes 196640 | tf_op jit(solution)/shard_map/ppermute | solution.py:20
  119.6 5.4 %collective-permute-done.18 = f32[96,512]{1,0:T(8,128)S(1)} collective-permute-done((f32[96,512]{1,0:T(8,128)S(1)}, f32[96,512]{1,0:T(8,128)S(1)}, u32[]{:S(2)}, u32[]{:S(2)}) %collective-permute-start.18) | collective-permute-done | bytes 196640 | tf_op jit(solution)/shard_map/ppermute | solution.py:20
  125.1 3.8 %collective-permute-start.19 = (f32[96,512]{1,0:T(8,128)S(1)}, f32[96,512]{1,0:T(8,128)S(1)}, u32[]{:S(2)}, u32[]{:S(2)}) collective-permute-start(f32[96,512]{1,0:T(8,128)S(1)} %add.339), channel_id=1, source_target_pairs={{0,1},{1,0},{2,3},{3,2},{4,5},{5,4},{6,7},{7,6},{8,9},{9,8},{10,11... | collective-permute-start | bytes 589832 | tf_op jit(solution)/shard_map/ppermute | solution.py:20
  128.9 3.6 %collective-permute-done.19 = f32[96,512]{1,0:T(8,128)S(1)} collective-permute-done((f32[96,512]{1,0:T(8,128)S(1)}, f32[96,512]{1,0:T(8,128)S(1)}, u32[]{:S(2)}, u32[]{:S(2)}) %collective-permute-start.19) | collective-permute-done | bytes 196640 | tf_op jit(solution)/shard_map/ppermute | solution.py:20
  133.6 6.8 %collective-permute-done.22 = f32[96,512]{1,0:T(8,128)S(1)} collective-permute-done((f32[96,512]{1,0:T(8,128)S(1)}, f32[96,512]{1,0:T(8,128)S(1)}, u32[]{:S(2)}, u32[]{:S(2)}) %collective-permute-start.22) | collective-permute-done | bytes 196640 | tf_op jit(solution)/shard_map/ppermute | solution.py:20
  141.8 6.5 %collective-permute-done.23 = f32[192,512]{1,0:T(8,128)S(1)} collective-permute-done((f32[192,512]{1,0:T(8,128)S(1)}, f32[192,512]{1,0:T(8,128)S(1)}, u32[]{:S(2)}, u32[]{:S(2)}) %collective-permute-start.23) | collective-permute-done | bytes 393248 | tf_op jit(solution)/shard_map/ppermute | solution.py:20
  151.8 6.8 %power.1.v_ref = f32[128,512]{1,0:T(8,128)S(1)} custom-call(s32[1]{0:T(128)} %bitcast.5.refs_1_.refs_0_, f32[384,512]{1,0:T(8,128)S(1)} %maximum_select_fusion.refs_1_, f32[384,512]{1,0:T(8,128)S(1)} %maximum_select_fusion.1.refs_2_, f32[384,512]{1,0:T(8,128)S(1)} %collective-permute-done.24.refs_3_, f32[384,512]{1,0:T(8,128)S(1)} %collective-permute-done.25.refs_4_, ...), custom_call_target="tpu_custom_call" | custom-call | flops 3623878656 | bytes 4194304 | tf_op jit(solution)/shard_map/power/pallas_call | solution.py:307
  164.2 7.2 %collective-permute-done.26 = f32[2,64,768]{2,1,0:T(8,128)S(1)} collective-permute-done((f32[2,64,768]{2,1,0:T(8,128)S(1)}, f32[2,64,768]{2,1,0:T(8,128)S(1)}, u32[]{:S(2)}, u32[]{:S(2)}) %collective-permute-start.26) | collective-permute-done | bytes 393248 | tf_op jit(solution)/shard_map/ppermute | solution.py:34
  178.1 3.2 %collective-permute-done.28.refs_2_ = f32[2,48,256]{2,1,0:T(8,128)S(1)} collective-permute-done((f32[2,48,256]{2,1,0:T(8,128)S(1)}, f32[2,48,256]{2,1,0:T(8,128)S(1)}, u32[]{:S(2)}, u32[]{:S(2)}) %collective-permute-start.28) | collective-permute-done | bytes 98336 | tf_op jit(solution)/shard_map/ppermute | solution.py:20
  181.3 2.7 %dft.1 = f32[2,48,1024]{2,1,0:T(8,128)} custom-call(s32[4]{0:T(128)S(1)} %copy-done.13, f32[2,48,256]{2,1,0:T(8,128)S(1)} %bitcast.44, f32[2,48,256]{2,1,0:T(8,128)S(1)} %collective-permute-done.27.refs_1_, f32[2,48,256]{2,1,0:T(8,128)S(1)} %collective-permute-done.28.refs_2_, f32[2,48,256]{2,1,0:T(8,128)S(1)} %collective-permute-done.29.refs_3_, ...), custom_call_target="tpu_custom_call" | custom-call | tf_op jit(solution)/shard_map/dft/pallas_call | solution.py:395
  (123 shorter events, 49.4 us)
Async XLA Ops:
  3.5 15.0 %collective-permute-start.6 = (f32[2,136,256]{2,1,0:T(8,128)}, f32[2,136,256]{2,1,0:T(8,128)S(1)}, u32[]{:S(2)}, u32[]{:S(2)}) collective-permute-start(f32[2,136,256]{2,1,0:T(8,128)} %get-tuple-element.31), channel_id=1, source_target_pairs={{0,1},{1,0},{2,3},{3,2},{4,5},{5,4},{6,7},{7,6},{8,9},{9,8},{10,11... | collective-permute-start | bytes 835592 | tf_op jit(solution)/shard_map/ppermute | solution.py:20
  5.1 22.7 %collective-permute-start.7 = (f32[2,136,256]{2,1,0:T(8,128)}, f32[2,136,256]{2,1,0:T(8,128)}, u32[]{:S(2)}, u32[]{:S(2)}) collective-permute-start(f32[2,136,256]{2,1,0:T(8,128)} %get-tuple-element.32), channel_id=1, source_target_pairs={{0,2},{1,3},{2,0},{3,1},{4,6},{5,7},{6,4},{7,5},{8,10},{9,11},{10,... | collective-permute-start | bytes 835592 | tf_op jit(solution)/shard_map/ppermute | solution.py:20
  7.7 20.8 %collective-permute-start.8 = (f32[2,136,256]{2,1,0:T(8,128)}, f32[2,136,256]{2,1,0:T(8,128)}, u32[]{:S(2)}, u32[]{:S(2)}) collective-permute-start(f32[2,136,256]{2,1,0:T(8,128)} %get-tuple-element.33), channel_id=1, source_target_pairs={{0,3},{1,2},{2,1},{3,0},{4,7},{5,6},{6,5},{7,4},{8,11},{9,10},{10,... | collective-permute-start | bytes 835592 | tf_op jit(solution)/shard_map/ppermute | solution.py:20
  10.6 48.9 %collective-permute-start.3 = (f32[2,128,256]{2,1,0:T(8,128)}, f32[2,128,256]{2,1,0:T(8,128)S(1)}, u32[]{:S(2)}, u32[]{:S(2)}) collective-permute-start(f32[2,128,256]{2,1,0:T(8,128)} %get-tuple-element.58), channel_id=1, source_target_pairs={{0,1},{1,0},{2,3},{3,2},{4,5},{5,4},{6,7},{7,6},{8,9},{9,8},{10,11... | collective-permute-start | bytes 786440 | tf_op jit(solution)/shard_map/ppermute | solution.py:20
  11.3 49.6 %collective-permute-start.4 = (f32[2,128,256]{2,1,0:T(8,128)}, f32[2,128,256]{2,1,0:T(8,128)}, u32[]{:S(2)}, u32[]{:S(2)}) collective-permute-start(f32[2,128,256]{2,1,0:T(8,128)} %get-tuple-element.57), channel_id=1, source_target_pairs={{0,2},{1,3},{2,0},{3,1},{4,6},{5,7},{6,4},{7,5},{8,10},{9,11},{10,... | collective-permute-start | bytes 786440 | tf_op jit(solution)/shard_map/ppermute | solution.py:20
  18.5 42.4 %collective-permute-start.5 = (f32[2,128,256]{2,1,0:T(8,128)}, f32[2,128,256]{2,1,0:T(8,128)}, u32[]{:S(2)}, u32[]{:S(2)}) collective-permute-start(f32[2,128,256]{2,1,0:T(8,128)} %get-tuple-element.56), channel_id=1, source_target_pairs={{0,3},{1,2},{2,1},{3,0},{4,7},{5,6},{6,5},{7,4},{8,11},{9,10},{10,... | collective-permute-start | bytes 786440 | tf_op jit(solution)/shard_map/ppermute | solution.py:20
  27.8 38.3 %collective-permute-start = (f32[2,128,256]{2,1,0:T(8,128)}, f32[2,128,256]{2,1,0:T(8,128)}, u32[]{:S(2)}, u32[]{:S(2)}) collective-permute-start(f32[2,128,256]{2,1,0:T(8,128)} %get-tuple-element.62), channel_id=1, source_target_pairs={{0,1},{1,0},{2,3},{3,2},{4,5},{5,4},{6,7},{7,6},{8,9},{9,8},{10,11... | collective-permute-start | bytes 786440 | tf_op jit(solution)/shard_map/ppermute | solution.py:20
  40.6 35.7 %collective-permute-start.1 = (f32[2,128,256]{2,1,0:T(8,128)S(1)}, f32[2,128,256]{2,1,0:T(8,128)S(1)}, u32[]{:S(2)}, u32[]{:S(2)}) collective-permute-start(f32[2,128,256]{2,1,0:T(8,128)S(1)} %copy-done.15), channel_id=1, source_target_pairs={{0,2},{1,3},{2,0},{3,1},{4,6},{5,7},{6,4},{7,5},{8,10},{9,11},{10,... | collective-permute-start | bytes 786440 | tf_op jit(solution)/shard_map/ppermute | solution.py:20
  59.5 16.8 %collective-permute-start.2 = (f32[2,128,256]{2,1,0:T(8,128)S(1)}, f32[2,128,256]{2,1,0:T(8,128)S(1)}, u32[]{:S(2)}, u32[]{:S(2)}) collective-permute-start(f32[2,128,256]{2,1,0:T(8,128)S(1)} %copy-done.14), channel_id=1, source_target_pairs={{0,3},{1,2},{2,1},{3,0},{4,7},{5,6},{6,5},{7,4},{8,11},{9,10},{10,... | collective-permute-start | bytes 786440 | tf_op jit(solution)/shard_map/ppermute | solution.py:20
  86.1 11.2 %collective-permute-start.13 = (f32[192,512]{1,0:T(8,128)S(1)}, f32[192,512]{1,0:T(8,128)S(1)}, u32[]{:S(2)}, u32[]{:S(2)}) collective-permute-start(f32[192,512]{1,0:T(8,128)S(1)} %get-tuple-element.42), channel_id=1, source_target_pairs={{0,8},{4,12},{8,0},{12,4},{16,24},{20,28},{24,16},{28,20},{1,9},{5... | collective-permute-start | bytes 1179656 | tf_op jit(solution)/shard_map/ppermute | solution.py:20
  87.7 10.9 %collective-permute-start.14 = (f32[192,512]{1,0:T(8,128)S(1)}, f32[192,512]{1,0:T(8,128)S(1)}, u32[]{:S(2)}, u32[]{:S(2)}) collective-permute-start(f32[192,512]{1,0:T(8,128)S(1)} %get-tuple-element.44), channel_id=1, source_target_pairs={{0,16},{4,20},{8,24},{12,28},{16,0},{20,4},{24,8},{28,12},{1,17},{... | collective-permute-start | bytes 1179656 | tf_op jit(solution)/shard_map/ppermute | solution.py:20
  100.6 6.0 %collective-permute-start.15 = (f32[96,512]{1,0:T(8,128)}, f32[96,512]{1,0:T(8,128)S(1)}, u32[]{:S(2)}, u32[]{:S(2)}) collective-permute-start(f32[96,512]{1,0:T(8,128)} %get-tuple-element.46), channel_id=1, source_target_pairs={{0,16},{4,20},{8,24},{12,28},{16,0},{20,4},{24,8},{28,12},{1,17},{... | collective-permute-start | bytes 589832 | tf_op jit(solution)/shard_map/ppermute | solution.py:20
  102.1 5.9 %collective-permute-start.16 = (f32[96,512]{1,0:T(8,128)}, f32[96,512]{1,0:T(8,128)S(1)}, u32[]{:S(2)}, u32[]{:S(2)}) collective-permute-start(f32[96,512]{1,0:T(8,128)} %get-tuple-element.48), channel_id=1, source_target_pairs={{0,8},{4,12},{8,0},{12,4},{16,24},{20,28},{24,16},{28,20},{1,9},{5... | collective-permute-start | bytes 589832 | tf_op jit(solution)/shard_map/ppermute | solution.py:20
  109.0 8.9 %collective-permute-start.17 = (f32[96,512]{1,0:T(8,128)S(1)}, f32[96,512]{1,0:T(8,128)S(1)}, u32[]{:S(2)}, u32[]{:S(2)}) collective-permute-start(f32[96,512]{1,0:T(8,128)S(1)} %get-tuple-element.50), channel_id=1, source_target_pairs={{0,1},{1,0},{2,3},{3,2},{4,5},{5,4},{6,7},{7,6},{8,9},{9,8},{10,11... | collective-permute-start | bytes 589832 | tf_op jit(solution)/shard_map/ppermute | solution.py:20
  117.9 7.2 %collective-permute-start.18 = (f32[96,512]{1,0:T(8,128)S(1)}, f32[96,512]{1,0:T(8,128)S(1)}, u32[]{:S(2)}, u32[]{:S(2)}) collective-permute-start(f32[96,512]{1,0:T(8,128)S(1)} %add.338), channel_id=1, source_target_pairs={{0,2},{1,3},{2,0},{3,1},{4,6},{5,7},{6,4},{7,5},{8,10},{9,11},{10,... | collective-permute-start | bytes 589832 | tf_op jit(solution)/shard_map/ppermute | solution.py:20
  125.1 7.4 %collective-permute-start.19 = (f32[96,512]{1,0:T(8,128)S(1)}, f32[96,512]{1,0:T(8,128)S(1)}, u32[]{:S(2)}, u32[]{:S(2)}) collective-permute-start(f32[96,512]{1,0:T(8,128)S(1)} %add.339), channel_id=1, source_target_pairs={{0,1},{1,0},{2,3},{3,2},{4,5},{5,4},{6,7},{7,6},{8,9},{9,8},{10,11... | collective-permute-start | bytes 589832 | tf_op jit(solution)/shard_map/ppermute | solution.py:20
  132.6 7.8 %collective-permute-start.22 = (f32[96,512]{1,0:T(8,128)S(1)}, f32[96,512]{1,0:T(8,128)S(1)}, u32[]{:S(2)}, u32[]{:S(2)}) collective-permute-start(f32[96,512]{1,0:T(8,128)S(1)} %get-tuple-element.79), channel_id=1, source_target_pairs={{0,8},{4,12},{8,0},{12,4},{16,24},{20,28},{24,16},{28,20},{1,9},{5... | collective-permute-start | bytes 589832 | tf_op jit(solution)/shard_map/ppermute | solution.py:20
  133.1 7.9 %collective-permute-start.20 = (f32[96,512]{1,0:T(8,128)S(1)}, f32[96,512]{1,0:T(8,128)S(1)}, u32[]{:S(2)}, u32[]{:S(2)}) collective-permute-start(f32[96,512]{1,0:T(8,128)S(1)} %get-tuple-element.80), channel_id=1, source_target_pairs={{0,16},{4,20},{8,24},{12,28},{16,0},{20,4},{24,8},{28,12},{1,17},{... | collective-permute-start | bytes 589832 | tf_op jit(solution)/shard_map/ppermute | solution.py:20
  140.4 7.8 %collective-permute-start.23 = (f32[192,512]{1,0:T(8,128)S(1)}, f32[192,512]{1,0:T(8,128)S(1)}, u32[]{:S(2)}, u32[]{:S(2)}) collective-permute-start(f32[192,512]{1,0:T(8,128)S(1)} %maximum_select_fusion.3), channel_id=1, source_target_pairs={{0,16},{4,20},{8,24},{12,28},{16,0},{20,4},{24,8},{28,12},{1,17},{... | collective-permute-start | bytes 1179656 | tf_op jit(solution)/shard_map/ppermute | solution.py:20
  141.0 7.8 %collective-permute-start.21 = (f32[192,512]{1,0:T(8,128)S(1)}, f32[192,512]{1,0:T(8,128)S(1)}, u32[]{:S(2)}, u32[]{:S(2)}) collective-permute-start(f32[192,512]{1,0:T(8,128)S(1)} %maximum_select_fusion.2), channel_id=1, source_target_pairs={{0,8},{4,12},{8,0},{12,4},{16,24},{20,28},{24,16},{28,20},{1,9},{5... | collective-permute-start | bytes 1179656 | tf_op jit(solution)/shard_map/ppermute | solution.py:20
  161.4 10.0 %collective-permute-start.26 = (f32[2,64,768]{2,1,0:T(8,128)S(1)}, f32[2,64,768]{2,1,0:T(8,128)S(1)}, u32[]{:S(2)}, u32[]{:S(2)}) collective-permute-start(f32[2,64,768]{2,1,0:T(8,128)S(1)} %beams.1), channel_id=1, source_target_pairs={{0,4},{4,8},{8,12},{12,16},{16,20},{20,24},{24,28},{1,5},{5,9},{9,... | collective-permute-start | bytes 1179656 | tf_op jit(solution)/shard_map/ppermute | solution.py:34
  171.6 6.5 %collective-permute-start.27 = (f32[2,48,256]{2,1,0:T(8,128)S(1)}, f32[2,48,256]{2,1,0:T(8,128)S(1)}, u32[]{:S(2)}, u32[]{:S(2)}) collective-permute-start(f32[2,48,256]{2,1,0:T(8,128)S(1)} %bitcast.46), channel_id=1, source_target_pairs={{0,1},{1,0},{2,3},{3,2},{4,5},{5,4},{6,7},{7,6},{8,9},{9,8},{10,11... | collective-permute-start | bytes 294920 | tf_op jit(solution)/shard_map/ppermute | solution.py:20
  173.2 8.0 %collective-permute-start.28 = (f32[2,48,256]{2,1,0:T(8,128)S(1)}, f32[2,48,256]{2,1,0:T(8,128)S(1)}, u32[]{:S(2)}, u32[]{:S(2)}) collective-permute-start(f32[2,48,256]{2,1,0:T(8,128)S(1)} %bitcast.47), channel_id=1, source_target_pairs={{0,2},{1,3},{2,0},{3,1},{4,6},{5,7},{6,4},{7,5},{8,10},{9,11},{10,... | collective-permute-start | bytes 294920 | tf_op jit(solution)/shard_map/ppermute | solution.py:20
  174.2 7.1 %collective-permute-start.29 = (f32[2,48,256]{2,1,0:T(8,128)S(1)}, f32[2,48,256]{2,1,0:T(8,128)S(1)}, u32[]{:S(2)}, u32[]{:S(2)}) collective-permute-start(f32[2,48,256]{2,1,0:T(8,128)S(1)} %bitcast.48), channel_id=1, source_target_pairs={{0,3},{1,2},{2,1},{3,0},{4,7},{5,6},{6,5},{7,4},{8,11},{9,10},{10,... | collective-permute-start | bytes 294920 | tf_op jit(solution)/shard_map/ppermute | solution.py:20
  (22 other events, 204.1 us)
